TPU v7x, 32 devices: a whole 2x2x4 slice. The times are simulated.
32 devices in a mesh: fsdp: 8 (over z, x), side: 4 (over y, core).
Axes of the slice: x: 2, y: 2, z: 4, core: 2. Of those that a mesh axis runs over, the one named last changes fastest.
Arguments:
- attn_inputs: bfloat16 [4096, 5120], P(('side', 'fsdp')), may hold values from -6 to 6
- queries: bfloat16 [4096, 2560], P(('side', 'fsdp')), may hold values from -310 to 310
- key_vectors: bfloat16 [4096, 512], P(('side', 'fsdp')), may hold values from -12 to 12
- logp_grad: bfloat16 [4096, 2560], P(('side', 'fsdp')), may hold values from -24 to 24
- new_logp: float32 [4096], P(('side', 'fsdp')), may hold values from -6.5 to -0.01
- old_logp: float32 [4096], P(('side', 'fsdp')), may hold values from -4 to -0.05
- rewards: float32 [8], replicated, may hold values from -8 to 8
- group_ids: int32 [8], replicated, may hold values from 0 to 1
- lengths: int32 [8], replicated, may hold values from 256 to 512
- value_proj: bfloat16 [5120, 512], P('fsdp'), may hold values from -0.078125 to 0.078125
- first_moment: bfloat16 [5120, 512], P(('fsdp', 'side')), may hold values from -120 to 120
- second_moment: bfloat16 [5120, 512], P(('fsdp', 'side')), may hold values from 100 to 9984
Outputs:
- input_grad: bfloat16 [4096, 5120], P(('side', 'fsdp'))
- new_proj: bfloat16 [5120, 512], P('fsdp')
- new_first: bfloat16 [5120, 512], P(('fsdp', 'side'))
- new_second: bfloat16 [5120, 512], P(('fsdp', 'side'))
All inputs are finite; a program needn't handle non-finite values.
Results may differ from a plain program's by a relative error of at most 0.03.
Values may be sent and summed in bfloat16 or wider, within the bound.
No kernel may reach another device: no remote copies, remote signals or barrier semaphores. Data moves between devices by JAX's collectives and lax.ppermute only.
A program may use at most 64 MiB of HBM per device.

v0:
```python
import functools
import math

import jax
import jax.numpy as jnp
from jax import lax
from jax.experimental import pallas as pl
from jax.experimental.pallas import tpu as pltpu
from jax.sharding import Mesh
from jax.sharding import PartitionSpec as P


HEAD = 128
ROLLS = 2
PAIR = 2


clip_low = 0.8
clip_high = 1.2
decay_first = 0.9
decay_second = 0.95
step_rate = 0.001
weight_decay = 0.1
adam_eps = 1e-08
bias_first = 1.0 - 0.9**10
bias_second = 1.0 - 0.95**10


def advantages(rewards, group_ids):
    same = (group_ids[:, None] == group_ids[None, :]).astype(jnp.float32)
    counts = jnp.sum(same, axis=1)
    own_mean = jnp.sum(same * rewards[None, :], axis=1) / counts
    spread = rewards - own_mean
    variance = jnp.sum(same * (spread * spread)[None, :], axis=1) / counts
    return spread / jnp.maximum(jnp.sqrt(variance), 1.0)


def coefficient(new_lp, old_lp, adv_tok, len_tok, pos_tok, full_len):
    ratio_now = jnp.exp(new_lp - old_lp)
    clipped = jnp.clip(ratio_now, clip_low, clip_high)
    active = (ratio_now * adv_tok <= clipped * adv_tok) & (pos_tok < len_tok)
    len_weight = full_len / len_tok.astype(jnp.float32)
    return jnp.where(active, -adv_tok * ratio_now * len_weight, 0.0)


def attention_kernel(slots, half, place, q_own, q_far, g_own, g_far, c_own, c_far, *refs):
    key_refs, part_refs, probs = refs[:slots], refs[slots : 2 * slots], refs[2 * slots]
    z_index, x_index = place[0], place[1]
    per_group = q_own.shape[1] // HEAD
    block = PAIR * half
    scale = 1.0 / math.sqrt(HEAD)

    def spot(dim):
        at = lax.broadcasted_iota(jnp.int32, (block, block), dim)
        return jnp.where(at < half, at + x_index * half, at - half + (1 - x_index) * half)

    causal = spot(0) <= spot(1)
    for roll in range(ROLLS):
        rows = slice(roll * half, (roll + 1) * half)
        far_rows = slice((ROLLS + roll) * half, (ROLLS + roll + 1) * half)
        keys = jnp.concatenate(
            [key_refs[n][part, :] for n in range(slots) for part in (rows, far_rows)], axis=0
        )
        grads = []
        for head in range(per_group):
            cols = slice(head * HEAD, (head + 1) * HEAD)
            query = jnp.concatenate([q_own[rows, cols], q_far[rows, cols]], axis=0)
            grads += [
                (c[rows, :] * g[rows, cols].astype(jnp.float32)).astype(jnp.bfloat16)
                for c, g in ((c_own, g_own), (c_far, g_far))
            ]
            scores = (
                lax.dot_general(
                    keys, query, (((1,), (1,)), ((), ())), preferred_element_type=jnp.float32
                )
                * scale
            )
            pieces = [jnp.where(causal, scores[:block], -1e30)]
            for n in range(1, slots):
                pieces.append(
                    jnp.where(z_index >= n, scores[n * block : (n + 1) * block], -1e30)
                )
            top = functools.reduce(
                jnp.maximum, [jnp.max(piece, axis=0, keepdims=True) for piece in pieces]
            )
            expo = [jnp.exp(piece - top) for piece in pieces]
            total = sum(jnp.sum(piece, axis=0, keepdims=True) for piece in expo)
            inverse = 1.0 / total
            for n in range(slots):
                probs[n * block : (n + 1) * block, head * block : (head + 1) * block] = (
                    expo[n] * inverse
                ).astype(jnp.bfloat16)
        summed = jnp.dot(
            probs[...], jnp.concatenate(grads, axis=0), preferred_element_type=jnp.float32
        ).astype(jnp.bfloat16)
        for n in range(slots):
            part_refs[n][rows, :] = summed[n * block : n * block + half]
            part_refs[n][far_rows, :] = summed[n * block + half : (n + 1) * block]


def attention_parts(place, queries, q_far, logp_grad, g_far, c_own, c_far, key_blocks):
    slots = len(key_blocks)
    tok_rows, q_cols = q_far.shape
    kv_heads = key_blocks[0].shape[1] // HEAD
    per_head = q_cols // kv_heads
    half = tok_rows // ROLLS
    own_spec = pl.BlockSpec((tok_rows, per_head), lambda h, place: (0, place[1] * kv_heads + h))
    far_spec = pl.BlockSpec((tok_rows, per_head), lambda h, place: (0, h))
    coeff_spec = pl.BlockSpec((tok_rows, 1), lambda h, place: (0, 0))
    k_spec = pl.BlockSpec((PAIR * tok_rows, HEAD), lambda h, place: (0, h))
    shape = jax.ShapeDtypeStruct(key_blocks[0].shape, jnp.bfloat16)
    work = 4 * kv_heads * per_head * ROLLS * (PAIR * half) ** 2 * slots
    return pl.pallas_call(
        functools.partial(attention_kernel, slots, half),
        grid_spec=pltpu.PrefetchScalarGridSpec(
            num_scalar_prefetch=1,
            grid=(kv_heads,),
            in_specs=[own_spec, far_spec] * 2 + [coeff_spec] * 2 + [k_spec] * slots,
            out_specs=[k_spec] * slots,
            scratch_shapes=[
                pltpu.VMEM(
                    (slots * PAIR * half, per_head // HEAD * PAIR * half), jnp.bfloat16
                )
            ],
        ),
        out_shape=[shape] * slots,
        cost_estimate=pl.CostEstimate(
            flops=work, bytes_accessed=8 * tok_rows * q_cols, transcendentals=work // 256
        ),
    )(place, queries, q_far, logp_grad, g_far, c_own, c_far, *key_blocks)


def pack_kernel(place, k_own, k_far, q_far, g_far, *outs):
    for source, out in zip((k_own, k_far, q_far, g_far), outs):
        out[...] = source[...]


def packed(place, key_vectors, queries, logp_grad):
    tok_rows = queries.shape[0]
    steps = key_vectors.shape[1] // HEAD // PAIR
    q_cols = queries.shape[1] // PAIR // steps

    def spec(cols, far):
        def where(h, place):
            x = 1 - place[1] if far else place[1]
            return 0, x * steps + h

        return pl.BlockSpec((tok_rows, cols), where)

    def half(cols):
        return jax.ShapeDtypeStruct((tok_rows, steps * cols), jnp.bfloat16)

    return pl.pallas_call(
        pack_kernel,
        grid_spec=pltpu.PrefetchScalarGridSpec(
            num_scalar_prefetch=1,
            grid=(steps,),
            in_specs=[spec(HEAD, False), spec(HEAD, True), spec(q_cols, True), spec(q_cols, True)],
            out_specs=[
                pl.BlockSpec((tok_rows, cols), lambda h, place: (0, h))
                for cols in (HEAD, HEAD, q_cols, q_cols)
            ],
        ),
        out_shape=[half(HEAD), half(HEAD), half(q_cols), half(q_cols)],
        cost_estimate=pl.CostEstimate(
            flops=0, bytes_accessed=8 * tok_rows * steps * q_cols, transcendentals=0
        ),
    )(place, key_vectors, key_vectors, queries, logp_grad)


def owner_kernel(z_size, pieces, place, near, far, *refs):
    values, outs = refs[: 2 * pieces], refs[2 * pieces :]
    sources = [(c, y) for c in range(near.shape[0]) for y in range(near.shape[1])]
    first = jnp.concatenate([ref[...] for ref in values[:pieces]], axis=0)
    second = jnp.concatenate([ref[...] for ref in values[pieces:]], axis=0)
    half = first.shape[1]
    for k in range(z_size):
        owner = place[0] + k
        owner = jnp.where(owner >= z_size, owner - z_size, owner)
        near_cols = [near[c, y, owner] for c, y in sources]
        far_cols = [far[c, y, owner] for c, y in sources]
        own_first = [cols for pair in zip(near_cols, far_cols) for cols in pair]
        far_first = [cols for pair in zip(far_cols, near_cols) for cols in pair]
        outs[k][:, :half] = jnp.dot(
            jnp.concatenate(own_first, axis=1), first, preferred_element_type=jnp.float32
        ).astype(jnp.bfloat16)
        outs[k][:, half:] = jnp.dot(
            jnp.concatenate(far_first, axis=1), second, preferred_element_type=jnp.float32
        ).astype(jnp.bfloat16)


def owner_products(place, near, far, first, second):
    _, _, z_size, rows, _ = near.shape
    pieces = len(first)
    width = 2 * first[0].shape[1]
    shape = jax.ShapeDtypeStruct((rows, width), jnp.bfloat16)
    whole = pl.BlockSpec(memory_space=pltpu.VMEM)
    return pl.pallas_call(
        functools.partial(owner_kernel, z_size, pieces),
        in_specs=[pl.BlockSpec(memory_space=pltpu.SMEM)] + [whole] * (2 + 2 * pieces),
        out_specs=[whole] * z_size,
        out_shape=[shape] * z_size,
        cost_estimate=pl.CostEstimate(
            flops=4 * near.size * width, bytes_accessed=8 * near.size, transcendentals=0
        ),
    )(place, near, far, *first, *second)


def row_kernel(z_size, y_size, place, *refs):
    ends = 2 * y_size, len(refs) - 1 - 2 * y_size
    values, proj, outs = refs[: ends[0]], refs[ends[0] : ends[1]], refs[ends[1] : -1]
    rows_all = refs[-1]
    rows, tok_rows = proj[0].shape[1], outs[0].shape[0]
    for c, ref in enumerate(proj):
        at_core = place[3] - c
        at_core = jnp.where(at_core < 0, at_core + len(proj), at_core)
        for k in range(z_size):
            at_z = place[0] - k
            at_z = jnp.where(at_z < 0, at_z + z_size, at_z)
            start = pl.multiple_of((at_z * len(proj) + at_core) * rows, rows)
            rows_all[pl.ds(start, rows), :] = ref[k]
    for y in range(y_size):
        first, second = values[y], values[y_size + y]
        own = [first[:tok_rows, :], second[tok_rows:, :]]
        far = [first[tok_rows:, :], second[:tok_rows, :]]
        for x, (low, high) in enumerate((own, far)):
            tokens = jnp.where(
                place[1] == 0,
                jnp.concatenate([low, high], axis=1),
                jnp.concatenate([high, low], axis=1),
            )
            outs[x * y_size + y][...] = lax.dot_general(
                tokens,
                rows_all[...],
                (((1,), (1,)), ((), ())),
                preferred_element_type=jnp.float32,
            ).astype(jnp.bfloat16)


def by_place(blocks, index):
    size = len(blocks)
    back = jnp.stack([blocks[-k % size] for k in range(size)])
    start = jnp.where(index == 0, 0, size - index)
    return lax.dynamic_slice_in_dim(jnp.concatenate([back, back], axis=0), start, size, 0)


def plain_row_products(place, first, second, proj):
    z_size, _, width = proj[0].shape
    tok_rows = first[0].shape[0] // PAIR
    cores = by_place(proj, place[3])
    along = by_place([cores[:, k] for k in range(z_size)], place[0])
    every = along.reshape(-1, width)
    outs = []
    for x in range(PAIR):
        for low, high in zip(first, second):
            near, far = slice(0, tok_rows), slice(tok_rows, PAIR * tok_rows)
            low, high = (low[near], high[far]) if x == 0 else (low[far], high[near])
            tokens = jnp.where(
                place[1] == 0,
                jnp.concatenate([low, high], axis=1),
                jnp.concatenate([high, low], axis=1),
            )
            outs.append(
                jnp.dot(tokens, every.T, preferred_element_type=jnp.float32).astype(jnp.bfloat16)
            )
    return outs


def row_products(place, first, second, proj):
    z_size, rows, width = proj[0].shape
    y_size = len(first)
    tok_rows = first[0].shape[0] // PAIR
    cols = z_size * len(proj) * rows
    if rows % 16 or cols % 128:
        return plain_row_products(place, first, second, proj)
    whole = pl.BlockSpec(memory_space=pltpu.VMEM)
    shape = jax.ShapeDtypeStruct((tok_rows, cols), jnp.bfloat16)
    return pl.pallas_call(
        functools.partial(row_kernel, z_size, y_size),
        in_specs=[pl.BlockSpec(memory_space=pltpu.SMEM)] + [whole] * (2 * y_size + len(proj)),
        out_specs=[whole] * (2 * y_size),
        out_shape=[shape] * (2 * y_size),
        scratch_shapes=[pltpu.VMEM((cols, width), jnp.bfloat16)],
        cost_estimate=pl.CostEstimate(
            flops=4 * y_size * tok_rows * width * cols,
            bytes_accessed=2 * cols * (width + 2 * y_size * tok_rows),
            transcendentals=0,
        ),
    )(place, *first, *second, *proj)


def final_kernel(z_size, place, *refs):
    pieces, out = refs[:-1], refs[-1]
    cols = pieces[0].shape[1] // z_size
    flags = place[1] == 0, place[2] == 0
    for z in range(z_size):
        part = slice(z * cols, (z + 1) * cols)
        near = [jnp.where(flags[1], pieces[y][:, part], pieces[1 - y][:, part]) for y in (0, 1)]
        far = [
            jnp.where(flags[1], pieces[2 + y][:, part], pieces[3 - y][:, part]) for y in (0, 1)
        ]
        near, far = jnp.concatenate(near, axis=1), jnp.concatenate(far, axis=1)
        wide = 2 * cols
        out[:, 2 * z * wide : (2 * z + 1) * wide] = jnp.where(flags[0], near, far)
        out[:, (2 * z + 1) * wide : (2 * z + 2) * wide] = jnp.where(flags[0], far, near)


def assembled(place, pieces, z_size):
    tokens = pieces[0].shape[0]
    y_size = len(pieces) // PAIR
    cols = pieces[0].shape[1] // z_size
    if y_size != 2 or 2 * cols % 128:
        split = [piece.reshape(tokens, z_size, cols) for piece in pieces]
        both = []
        for x in range(PAIR):
            found = jnp.stack(split[x * y_size : (x + 1) * y_size])
            start = jnp.where(place[2] == 0, 0, y_size - place[2])
            both.append(
                lax.dynamic_slice_in_dim(
                    jnp.concatenate([found, found], axis=0), start, y_size, 0
                )
            )
        both = jnp.stack(both)
        both = jnp.where(place[1] == 0, both, both[::-1])
        return both.transpose(2, 3, 0, 1, 4).reshape(tokens, -1)
    whole = pl.BlockSpec(memory_space=pltpu.VMEM)
    return pl.pallas_call(
        functools.partial(final_kernel, z_size),
        in_specs=[pl.BlockSpec(memory_space=pltpu.SMEM)] + [whole] * len(pieces),
        out_specs=whole,
        out_shape=jax.ShapeDtypeStruct((tokens, len(pieces) * z_size * cols), jnp.bfloat16),
        cost_estimate=pl.CostEstimate(
            flops=0, bytes_accessed=4 * tokens * len(pieces) * z_size * cols, transcendentals=0
        ),
    )(place, *pieces)


def adam_rows(old_rows, grad_rows, first_moment, second_moment):
    first = decay_first * first_moment.astype(jnp.float32) + (1.0 - decay_first) * grad_rows
    second = (
        decay_second * second_moment.astype(jnp.float32)
        + (1.0 - decay_second) * grad_rows * grad_rows
    )
    weight_now = old_rows.astype(jnp.float32)
    update = (
        first / bias_first / (jnp.sqrt(second / bias_second) + adam_eps) + weight_decay * weight_now
    )
    return (
        (weight_now - step_rate * update).astype(jnp.bfloat16),
        first.astype(jnp.bfloat16),
        second.astype(jnp.bfloat16),
    )


def shift(value, axis, step, wrap=True):
    size = lax.axis_size(axis)
    pairs = [(i, (i + step) % size) for i in range(size) if wrap or 0 <= i + step < size]
    return lax.ppermute(value, axis, pairs)


def turned(index, step, size):
    moved = index + step
    return jnp.where(moved >= size, moved - size, moved)


def cut(value, index, dim):
    return lax.dynamic_index_in_dim(value, index, dim, keepdims=False)


def step(
    attn_inputs,
    queries,
    key_vectors,
    logp_grad,
    new_logp,
    old_logp,
    rewards,
    group_ids,
    lengths,
    value_proj,
    first_moment,
    second_moment,
):
    z_size, y_size, core_size = lax.axis_size("z"), lax.axis_size("y"), lax.axis_size("core")
    z_index, x_index = lax.axis_index("z"), lax.axis_index("x")
    side_index = lax.axis_index("y") * core_size + lax.axis_index("core")
    tok_rows, _ = attn_inputs.shape
    half = tok_rows // ROLLS
    full_len = half * z_size * PAIR
    width = key_vectors.shape[1]
    shard_rows = first_moment.shape[0]
    y_index, core_index = lax.axis_index("y"), lax.axis_index("core")
    place = jnp.stack([z_index, x_index, y_index, core_index]).astype(jnp.int32)

    key_own, key_out, q_out, g_out = packed(place, key_vectors, queries, logp_grad)
    key_far = shift(key_out, "x", 1)
    q_far = shift(q_out, "x", 1)
    g_far = shift(g_out, "x", 1)
    key_block = jnp.concatenate([key_own, key_far], axis=0)
    key_blocks = [key_block] + [shift(key_block, "z", k, False) for k in range(1, z_size)]

    columns = attn_inputs.T.reshape(z_size, PAIR, y_size, core_size, shard_rows, tok_rows)
    by_y = [cut(columns, y_index, 2)] + [
        shift(cut(columns, turned(y_index, k, y_size), 2), "y", k)
        for k in range(1, y_size)
    ]
    by_core = [
        jnp.stack([cut(block, core_index, 2) for block in by_y]),
        shift(jnp.stack([cut(block, 1 - core_index, 2) for block in by_y]), "core", 1),
    ]
    near_cols = jnp.stack([cut(block, x_index, 2) for block in by_core])
    far_cols = shift(jnp.stack([cut(block, 1 - x_index, 2) for block in by_core]), "x", 1)

    advantage = advantages(rewards, group_ids)
    rolls = jnp.arange(rewards.shape[0], dtype=jnp.int32)[None, :]
    mine = rolls == side_index * ROLLS + jnp.arange(ROLLS, dtype=jnp.int32)[:, None]
    adv_roll = jnp.sum(jnp.where(mine, advantage[None, :], 0.0), axis=1)
    len_roll = jnp.sum(jnp.where(mine, lengths[None, :], 0), axis=1)
    position = (z_index * PAIR + x_index) * half + jnp.arange(half, dtype=jnp.int32)
    coeff = coefficient(
        new_logp.reshape(ROLLS, half),
        old_logp.reshape(ROLLS, half),
        adv_roll[:, None],
        len_roll[:, None],
        position[None, :],
        full_len,
    ).reshape(tok_rows)
    coeff_far = shift(coeff, "x", 1)

    own_proj = lax.dynamic_slice_in_dim(value_proj, side_index * shard_rows, shard_rows, 0)
    own_proj = lax.optimization_barrier(own_proj)
    own_rows = jnp.stack([own_proj] + [shift(own_proj, "z", k) for k in range(1, z_size)])
    proj = [own_rows, shift(own_rows, "core", 1)]

    parts = attention_parts(
        place,
        queries,
        q_far,
        logp_grad,
        g_far,
        coeff.reshape(tok_rows, 1),
        coeff_far.reshape(tok_rows, 1),
        key_blocks,
    )
    total = parts[0].astype(jnp.float32)
    for k in range(1, z_size):
        arrived = shift(parts[k], "z", -k, False)
        total = total + arrived.astype(jnp.float32)

    def over_sides(value):
        found = [value] + [shift(value, "y", k) for k in range(1, y_size)]
        return found + [shift(block, "core", 1) for block in found]

    first_cols = total.astype(jnp.bfloat16)
    second_cols = shift(first_cols, "x", 1)
    first_all = over_sides(first_cols)
    second_all = over_sides(second_cols)

    pieces = owner_products(place, near_cols, far_cols, first_all, second_all)
    arrived = [shift(pieces[k], "z", k) for k in range(1, z_size)]
    shard_grad = pieces[0].astype(jnp.float32)
    for piece in arrived:
        shard_grad = shard_grad + piece.astype(jnp.float32)

    products = row_products(place, first_all[:y_size], second_all[:y_size], proj)
    found = list(products)
    for k in range(1, y_size):
        found[k] = shift(products[k], "y", -k)
    found[y_size] = shift(products[y_size], "x", 1)
    for k in range(1, y_size):
        pairs = [
            (x * y_size + y, (1 - x) * y_size + (y - k) % y_size)
            for x in range(PAIR)
            for y in range(y_size)
        ]
        found[y_size + k] = lax.ppermute(products[y_size + k], ("x", "y"), pairs)
    input_grad = assembled(place, found, z_size)

    swap = jnp.concatenate([shard_grad[:, width // 2 :], shard_grad[:, : width // 2]], axis=1)
    new_rows, new_first, new_second = adam_rows(
        own_proj, jnp.where(x_index == 0, shard_grad, swap), first_moment, second_moment
    )
    new_proj = lax.all_gather(new_rows, ("y", "core"), axis=0, tiled=True)
    return (input_grad, new_proj, new_first, new_second)


def solution(mesh):
    fsdp_size, side_size = mesh.shape["fsdp"], mesh.shape["side"]
    fine = Mesh(
        mesh.devices.reshape(fsdp_size // PAIR, PAIR, side_size // 2, 2),
        ("z", "x", "y", "core"),
    )
    tokens = ("y", "core", "z", "x")
    placed = (
        P(tokens, None),
        P(tokens, None),
        P(tokens, None),
        P(tokens, None),
        P(tokens),
        P(tokens),
        P(),
        P(),
        P(),
        P(("z", "x"), None),
        P(("z", "x", "y", "core"), None),
        P(("z", "x", "y", "core"), None),
    )
    return jax.shard_map(
        step,
        mesh=fine,
        in_specs=placed,
        out_specs=(
            P(tokens, None),
            P(("z", "x"), None),
            P(("z", "x", "y", "core"), None),
            P(("z", "x", "y", "core"), None),
        ),
        check_vma=False,
    )
```

profile of v0, /device:TPU:0, one launch (start us, length us, event | category | flops | bytes accessed | tf_op | source)
XLA Modules:
  0.0 123.5 jit_solution(18257749253390876818)
XLA Ops:
  0.7 1.1 copy-done
  1.7 3.1 %collective-permute-start.13 = (bf16[160,512]{1,0:T(8,128)(2,1)S(1)}, bf16[160,512]{1,0:T(8,128)(2,1)S(1)}, u32[]{:S(2)}, u32[]{:S(2)}) collective-permute-start(bf16[160,512]{1,0:T(8,128)(2,1)S(1)} %constant_dynamic-slice_fusion), channel_id=1, source_target_pairs={{0,8},{8,16},{16,24},{24,0},{1,9},{9,17},{17,25},{25,1},{2,10},{10... | collective-permute-start | bytes 491528 | tf_op jit(solution)/shard_map/ppermute | solution.py:358
  4.8 2.6 %collective-permute-start.14 = (bf16[160,512]{1,0:T(8,128)(2,1)S(1)}, bf16[160,512]{1,0:T(8,128)(2,1)S(1)}, u32[]{:S(2)}, u32[]{:S(2)}) collective-permute-start(bf16[160,512]{1,0:T(8,128)(2,1)S(1)} %constant_dynamic-slice_fusion), channel_id=1, source_target_pairs={{0,16},{8,24},{16,0},{24,8},{1,17},{9,25},{17,1},{25,9},{2,18},{10... | collective-permute-start | bytes 491528 | tf_op jit(solution)/shard_map/ppermute | solution.py:358
  7.4 1.8 %copy.28 = bf16[128,5120]{0,1:T(8,128)(2,1)S(1)} copy(bf16[128,5120]{1,0:T(8,128)(2,1)} %param.12) | data formatting | bytes 2621440 | tf_op args[0]
  9.3 1.6 %collective-permute-start.20 = (bf16[4,2,2,160,128]{4,3,2,1,0:T(8,128)(2,1)S(1)}, bf16[4,2,2,160,128]{4,3,2,1,0:T(8,128)(2,1)}, u32[]{:S(2)}, u32[]{:S(2)}) collective-permute-start(bf16[4,2,2,160,128]{4,3,2,1,0:T(8,128)(2,1)S(1)} %dynamic-slice_bitcast_fusion), channel_id=1, source_target_pairs={{0,2},{2,0},{1,3},{3,1},{4,6},{6,4},{5,7},{7,5},{8,10},{10,8},{9,1... | collective-permute-start | bytes 1966088 | tf_op jit(solution)/shard_map/ppermute | solution.py:358
  12.4 1.6 %collective-permute-start.2 = (f32[128]{0:T(128)S(1)}, f32[128]{0:T(128)S(1)}, u32[]{:S(2)}, u32[]{:S(2)}) collective-permute-start(f32[128]{0:T(128)S(1)} %and_select_fusion), channel_id=1, source_target_pairs={{0,4},{4,0},{1,5},{5,1},{2,6},{6,2},{3,7},{7,3},{8,12},{12,8},{9,1... | collective-permute-start | bytes 1544 | tf_op jit(solution)/shard_map/ppermute | solution.py:358
  14.5 2.7 %shard_map.147 = (bf16[128,256]{1,0:T(8,128)(2,1)}, bf16[128,256]{1,0:T(8,128)(2,1)}, bf16[128,1280]{1,0:T(8,128)(2,1)}, bf16[128,1280]{1,0:T(8,128)(2,1)}) custom-call(s32[4]{0:T(128)} %pad_add_fusion.place, bf16[128,512]{1,0:T(8,128)(2,1)} %k_far.1, bf16[128,512]{1,0:T(8,128)(2,1)} %k_far.1, bf16[128,2560]{1,0:T(8,128)(2,1)} %q_own.1, bf16[128,2560]{1,0:T(8,128)(2,1)} %g_own.1), custom_call_target="tpu_custom_call" | custom-call | bytes 1310720 | tf_op jit(solution)/shard_map/pallas_call | solution.py:153
  17.8 7.6 %collective-permute-done.20 = bf16[4,2,2,160,128]{4,3,2,1,0:T(8,128)(2,1)} collective-permute-done((bf16[4,2,2,160,128]{4,3,2,1,0:T(8,128)(2,1)S(1)}, bf16[4,2,2,160,128]{4,3,2,1,0:T(8,128)(2,1)}, u32[]{:S(2)}, u32[]{:S(2)}) %collective-permute-start.20) | collective-permute-done | bytes 655392 | tf_op jit(solution)/shard_map/ppermute | solution.py:358
  25.4 1.1 dynamic-slice_bitcast_fusion.5
  26.7 1.4 %collective-permute-start.15 = (bf16[160,512]{1,0:T(8,128)(2,1)S(1)}, bf16[160,512]{1,0:T(8,128)(2,1)S(1)}, u32[]{:S(2)}, u32[]{:S(2)}) collective-permute-start(bf16[160,512]{1,0:T(8,128)(2,1)S(1)} %constant_dynamic-slice_fusion), channel_id=1, source_target_pairs={{0,24},{8,0},{16,8},{24,16},{1,25},{9,1},{17,9},{25,17},{2,26},{10... | collective-permute-start | bytes 491528 | tf_op jit(solution)/shard_map/ppermute | solution.py:358
  28.1 1.5 %collective-permute-start = (bf16[128,1280]{1,0:T(8,128)(2,1)}, bf16[128,1280]{1,0:T(8,128)(2,1)S(1)}, u32[]{:S(2)}, u32[]{:S(2)}) collective-permute-start(bf16[128,1280]{1,0:T(8,128)(2,1)} %get-tuple-element.20), channel_id=1, source_target_pairs={{0,4},{4,0},{1,5},{5,1},{2,6},{6,2},{3,7},{7,3},{8,12},{12,8},{9,1... | collective-permute-start | bytes 983048 | tf_op jit(solution)/shard_map/ppermute | solution.py:358
  30.2 2.6 %collective-permute-start.4 = (bf16[256,256]{1,0:T(8,128)(2,1)S(1)}, bf16[256,256]{1,0:T(8,128)(2,1)S(1)}, u32[]{:S(2)}, u32[]{:S(2)}) collective-permute-start(bf16[256,256]{1,0:T(8,128)(2,1)S(1)} %constant_dynamic-update-slice_fusion.refs_0_), channel_id=1, source_target_pairs={{0,8},{8,16},{16,24},{1,9},{9,17},{17,25},{2,10},{10,18},{18,26},{... | collective-permute-start | bytes 393224 | tf_op jit(solution)/shard_map/ppermute | solution.py:358
  33.4 2.9 %collective-permute-start.5 = (bf16[256,256]{1,0:T(8,128)(2,1)S(1)}, bf16[256,256]{1,0:T(8,128)(2,1)}, u32[]{:S(2)}, u32[]{:S(2)}) collective-permute-start(bf16[256,256]{1,0:T(8,128)(2,1)S(1)} %constant_dynamic-update-slice_fusion.refs_0_), channel_id=1, source_target_pairs={{0,16},{8,24},{1,17},{9,25},{2,18},{10,26},{3,19},{11,27},{4,20},{... | collective-permute-start | bytes 393224 | tf_op jit(solution)/shard_map/ppermute | solution.py:358
  36.3 0.7 copy-done.20
  36.9 5.6 %collective-permute-start.6 = (bf16[256,256]{1,0:T(8,128)(2,1)S(1)}, bf16[256,256]{1,0:T(8,128)(2,1)}, u32[]{:S(2)}, u32[]{:S(2)}) collective-permute-start(bf16[256,256]{1,0:T(8,128)(2,1)S(1)} %constant_dynamic-update-slice_fusion.refs_0_), channel_id=1, source_target_pairs={{0,24},{1,25},{2,26},{3,27},{4,28},{5,29},{6,30},{7,31}} | collective-permute-start | bytes 393224 | tf_op jit(solution)/shard_map/ppermute | solution.py:358
  42.5 0.7 copy.26.c_own
  43.2 0.7 copy.27.c_far
  44.0 0.9 pad_maximum_fusion.refs_4_
  45.6 6.3 %shard_map.148 = (bf16[256,256]{1,0:T(8,128)(2,1)}, bf16[256,256]{1,0:T(8,128)(2,1)}, bf16[256,256]{1,0:T(8,128)(2,1)}, bf16[256,256]{1,0:T(8,128)(2,1)}) custom-call(s32[4]{0:T(128)} %pad_add_fusion.place, bf16[128,2560]{1,0:T(8,128)(2,1)} %q_own.1, bf16[128,1280]{1,0:T(8,128)(2,1)} %copy-done.16, bf16[128,2560]{1,0:T(8,128)(2,1)} %g_own.1, ...), custom_call_target="tpu_custom_call" | custom-call | flops 671088640 | bytes 1310720 | tf_op jit(solution)/shard_map/pallas_call | solution.py:113
  52.0 1.3 %collective-permute-start.7 = (bf16[256,256]{1,0:T(8,128)(2,1)}, bf16[256,256]{1,0:T(8,128)(2,1)S(1)}, u32[]{:S(2)}, u32[]{:S(2)}) collective-permute-start(bf16[256,256]{1,0:T(8,128)(2,1)} %get-tuple-element.25), channel_id=1, source_target_pairs={{8,0},{16,8},{24,16},{9,1},{17,9},{25,17},{10,2},{18,10},{26,18},{... | collective-permute-start | bytes 393224 | tf_op jit(solution)/shard_map/ppermute | solution.py:358
  53.3 1.3 %collective-permute-start.8 = (bf16[256,256]{1,0:T(8,128)(2,1)}, bf16[256,256]{1,0:T(8,128)(2,1)S(1)}, u32[]{:S(2)}, u32[]{:S(2)}) collective-permute-start(bf16[256,256]{1,0:T(8,128)(2,1)} %get-tuple-element.26), channel_id=1, source_target_pairs={{16,0},{24,8},{17,1},{25,9},{18,2},{26,10},{19,3},{27,11},{20,4},{... | collective-permute-start | bytes 393224 | tf_op jit(solution)/shard_map/ppermute | solution.py:358
  54.6 1.3 %collective-permute-start.9 = (bf16[256,256]{1,0:T(8,128)(2,1)}, bf16[256,256]{1,0:T(8,128)(2,1)S(1)}, u32[]{:S(2)}, u32[]{:S(2)}) collective-permute-start(bf16[256,256]{1,0:T(8,128)(2,1)} %get-tuple-element.27), channel_id=1, source_target_pairs={{24,0},{25,1},{26,2},{27,3},{28,4},{29,5},{30,6},{31,7}} | collective-permute-start | bytes 393224 | tf_op jit(solution)/shard_map/ppermute | solution.py:358
  56.0 1.2 dynamic-slice_bitcast_fusion.1
  57.2 1.5 %collective-permute-start.22 = (bf16[2,2,4,160,128]{4,3,2,1,0:T(8,128)(2,1)S(1)}, bf16[2,2,4,160,128]{4,3,2,1,0:T(8,128)(2,1)}, u32[]{:S(2)}, u32[]{:S(2)}) collective-permute-start(bf16[2,2,4,160,128]{4,3,2,1,0:T(8,128)(2,1)S(1)} %pad_maximum_fusion.3), channel_id=1, source_target_pairs={{0,4},{4,0},{1,5},{5,1},{2,6},{6,2},{3,7},{7,3},{8,12},{12,8},{9,1... | collective-permute-start | bytes 1966088 | tf_op jit(solution)/shard_map/ppermute | solution.py:358
  58.7 3.1 %collective-permute-done.7 = bf16[256,256]{1,0:T(8,128)(2,1)S(1)} collective-permute-done((bf16[256,256]{1,0:T(8,128)(2,1)}, bf16[256,256]{1,0:T(8,128)(2,1)S(1)}, u32[]{:S(2)}, u32[]{:S(2)}) %collective-permute-start.7) | collective-permute-done | bytes 131104 | tf_op jit(solution)/shard_map/ppermute | solution.py:358
  61.8 6.0 %collective-permute-done.8 = bf16[256,256]{1,0:T(8,128)(2,1)S(1)} collective-permute-done((bf16[256,256]{1,0:T(8,128)(2,1)}, bf16[256,256]{1,0:T(8,128)(2,1)S(1)}, u32[]{:S(2)}, u32[]{:S(2)}) %collective-permute-start.8) | collective-permute-done | bytes 131104 | tf_op jit(solution)/shard_map/ppermute | solution.py:358
  67.9 1.6 %collective-permute-start.11 = (bf16[256,256]{1,0:T(8,128)(2,1)S(1)}, bf16[256,256]{1,0:T(8,128)(2,1)S(1)}, u32[]{:S(2)}, u32[]{:S(2)}) collective-permute-start(bf16[256,256]{1,0:T(8,128)(2,1)S(1)} %add_convert_fusion.refs_0_), channel_id=1, source_target_pairs={{0,4},{4,0},{1,5},{5,1},{2,6},{6,2},{3,7},{7,3},{8,12},{12,8},{9,1... | collective-permute-start | bytes 393224 | tf_op jit(solution)/shard_map/ppermute | solution.py:358
  69.5 1.5 %collective-permute-start.10 = (bf16[256,256]{1,0:T(8,128)(2,1)S(1)}, bf16[256,256]{1,0:T(8,128)(2,1)S(1)}, u32[]{:S(2)}, u32[]{:S(2)}) collective-permute-start(bf16[256,256]{1,0:T(8,128)(2,1)S(1)} %add_convert_fusion.refs_0_), channel_id=1, source_target_pairs={{0,2},{2,0},{1,3},{3,1},{4,6},{6,4},{5,7},{7,5},{8,10},{10,8},{9,1... | collective-permute-start | bytes 393224 | tf_op jit(solution)/shard_map/ppermute | solution.py:358
  71.0 6.2 %collective-permute-done.11.refs_2_.refs_4_ = bf16[256,256]{1,0:T(8,128)(2,1)S(1)} collective-permute-done((bf16[256,256]{1,0:T(8,128)(2,1)S(1)}, bf16[256,256]{1,0:T(8,128)(2,1)S(1)}, u32[]{:S(2)}, u32[]{:S(2)}) %collective-permute-start.11) | collective-permute-done | bytes 131104 | tf_op jit(solution)/shard_map/ppermute | solution.py:358
  77.2 1.5 %collective-permute-start.12 = (bf16[256,256]{1,0:T(8,128)(2,1)S(1)}, bf16[256,256]{1,0:T(8,128)(2,1)S(1)}, u32[]{:S(2)}, u32[]{:S(2)}) collective-permute-start(bf16[256,256]{1,0:T(8,128)(2,1)S(1)} %collective-permute-done.11.refs_2_.refs_4_), channel_id=1, source_target_pairs={{0,2},{2,0},{1,3},{3,1},{4,6},{6,4},{5,7},{7,5},{8,10},{10,8},{9,1... | collective-permute-start | bytes 393224 | tf_op jit(solution)/shard_map/ppermute | solution.py:358
  78.7 3.5 %collective-permute-done.12.refs_3_.refs_5_ = bf16[256,256]{1,0:T(8,128)(2,1)S(1)} collective-permute-done((bf16[256,256]{1,0:T(8,128)(2,1)S(1)}, bf16[256,256]{1,0:T(8,128)(2,1)S(1)}, u32[]{:S(2)}, u32[]{:S(2)}) %collective-permute-start.12) | collective-permute-done | bytes 131104 | tf_op jit(solution)/shard_map/ppermute | solution.py:358
  82.3 0.6 copy-done.19
  82.9 4.2 %shard_map.149 = (bf16[128,1280]{1,0:T(8,128)(2,1)}, bf16[128,1280]{1,0:T(8,128)(2,1)}, bf16[128,1280]{1,0:T(8,128)(2,1)}, bf16[128,1280]{1,0:T(8,128)(2,1)}) custom-call(s32[4]{0:T(128)} %pad_add_fusion.place, bf16[256,256]{1,0:T(8,128)(2,1)} %copy-done.7, bf16[256,256]{1,0:T(8,128)(2,1)} %copy-done.18, bf16[256,256]{1,0:T(8,128)(2,1)} %copy-done.17, ...), custom_call_target="tpu_custom_call" | custom-call | flops 671088640 | bytes 2621440 | tf_op jit(solution)/shard_map/pallas_call | solution.py:278
  87.1 1.5 %collective-permute-start.17 = (bf16[128,1280]{1,0:T(8,128)(2,1)}, bf16[128,1280]{1,0:T(8,128)(2,1)S(1)}, u32[]{:S(2)}, u32[]{:S(2)}) collective-permute-start(bf16[128,1280]{1,0:T(8,128)(2,1)} %get-tuple-element.29), channel_id=1, source_target_pairs={{0,2},{2,0},{1,3},{3,1},{4,6},{6,4},{5,7},{7,5},{8,10},{10,8},{9,1... | collective-permute-start | bytes 983048 | tf_op jit(solution)/shard_map/ppermute | solution.py:358
  89.1 1.0 collective-permute-done.23.refs_2_
  90.3 1.5 %collective-permute-start.18 = (bf16[128,1280]{1,0:T(8,128)(2,1)}, bf16[128,1280]{1,0:T(8,128)(2,1)S(1)}, u32[]{:S(2)}, u32[]{:S(2)}) collective-permute-start(bf16[128,1280]{1,0:T(8,128)(2,1)} %get-tuple-element.30), channel_id=1, source_target_pairs={{0,4},{4,0},{1,5},{5,1},{2,6},{6,2},{3,7},{7,3},{8,12},{12,8},{9,1... | collective-permute-start | bytes 983048 | tf_op jit(solution)/shard_map/ppermute | solution.py:358
  92.3 0.9 pad_maximum_fusion.2.near
  93.2 3.1 %shard_map.151 = (bf16[160,512]{1,0:T(8,128)(2,1)}, bf16[160,512]{1,0:T(8,128)(2,1)}, bf16[160,512]{1,0:T(8,128)(2,1)}, bf16[160,512]{1,0:T(8,128)(2,1)}) custom-call(s32[4]{0:T(128)} %pad_add_fusion.place, bf16[2,2,4,160,128]{4,3,2,1,0:T(8,128)(2,1)} %pad_maximum_fusion.2.near, bf16[2,2,4,160,128]{4,3,2,1,0:T(8,128)(2,1)} %collective-permute-done.22.far, ...), custom_call_target="tpu_custom_call" | custom-call | flops 671088640 | bytes 2621440 | tf_op jit(solution)/shard_map/pallas_call | solution.py:198
  96.4 1.7 %collective-permute-start.27 = (bf16[160,512]{1,0:T(8,128)(2,1)}, bf16[160,512]{1,0:T(8,128)(2,1)S(1)}, u32[]{:S(2)}, u32[]{:S(2)}) collective-permute-start(bf16[160,512]{1,0:T(8,128)(2,1)} %get-tuple-element.33), channel_id=1, source_target_pairs={{0,8},{8,16},{16,24},{24,0},{1,9},{9,17},{17,25},{25,1},{2,10},{10... | collective-permute-start | bytes 491528 | tf_op jit(solution)/shard_map/ppermute | solution.py:358
  98.1 3.9 %collective-permute-start.28 = (bf16[160,512]{1,0:T(8,128)(2,1)}, bf16[160,512]{1,0:T(8,128)(2,1)S(1)}, u32[]{:S(2)}, u32[]{:S(2)}) collective-permute-start(bf16[160,512]{1,0:T(8,128)(2,1)} %get-tuple-element.34), channel_id=1, source_target_pairs={{0,16},{8,24},{16,0},{24,8},{1,17},{9,25},{17,1},{25,9},{2,18},{10... | collective-permute-start | bytes 491528 | tf_op jit(solution)/shard_map/ppermute | solution.py:358
  102.0 5.5 %collective-permute-done.19.refs_3_ = bf16[128,1280]{1,0:T(8,128)(2,1)S(1)} collective-permute-done((bf16[128,1280]{1,0:T(8,128)(2,1)}, bf16[128,1280]{1,0:T(8,128)(2,1)S(1)}, u32[]{:S(2)}, u32[]{:S(2)}) %collective-permute-start.19) | collective-permute-done | bytes 327712 | tf_op jit(solution)/shard_map/ppermute | solution.py:476
  107.5 0.7 copy-done.4
  108.2 2.7 %shard_map.150 = bf16[128,5120]{1,0:T(8,128)(2,1)} custom-call(s32[4]{0:T(128)} %pad_add_fusion.place, bf16[128,1280]{1,0:T(8,128)(2,1)} %get-tuple-element.28.refs_0_, bf16[128,1280]{1,0:T(8,128)(2,1)} %copy-done.2, bf16[128,1280]{1,0:T(8,128)(2,1)} %copy-done.3, bf16[128,1280]{1,0:T(8,128)(2,1)} %copy-done.4), custom_call_target="tpu_custom_call" | custom-call | bytes 2621440 | tf_op jit(solution)/shard_map/pallas_call | solution.py:327
  110.9 2.0 %collective-permute-done.28 = bf16[160,512]{1,0:T(8,128)(2,1)S(1)} collective-permute-done((bf16[160,512]{1,0:T(8,128)(2,1)}, bf16[160,512]{1,0:T(8,128)(2,1)S(1)}, u32[]{:S(2)}, u32[]{:S(2)}) %collective-permute-start.28) | collective-permute-done | bytes 163872 | tf_op jit(solution)/shard_map/ppermute | solution.py:358
  113.0 0.7 fusion.9
  113.8 1.0 fusion.8
  114.7 7.9 %all_gather.3 = bf16[640,512]{1,0:T(8,128)(2,1)S(1)} all-gather(bf16[160,512]{1,0:T(8,128)(2,1)S(1)} %get-tuple-element.51), channel_id=1, replica_groups=mesh['z'=4,'x'=2,'y'=2,'core'=2] {'y','core'}, dimensions={0}, use_global_device_ids=true | all-gather | bytes 819200 | tf_op jit(solution)/shard_map/all_gather | solution.py:483
  122.6 0.8 copy.31
  (109 shorter events, 6.3 us)
Async XLA Ops:
  1.7 27.9 %collective-permute-start.13 = (bf16[160,512]{1,0:T(8,128)(2,1)S(1)}, bf16[160,512]{1,0:T(8,128)(2,1)S(1)}, u32[]{:S(2)}, u32[]{:S(2)}) collective-permute-start(bf16[160,512]{1,0:T(8,128)(2,1)S(1)} %constant_dynamic-slice_fusion), channel_id=1, source_target_pairs={{0,8},{8,16},{16,24},{24,0},{1,9},{9,17},{17,25},{25,1},{2,10},{10... | collective-permute-start | bytes 491528 | tf_op jit(solution)/shard_map/ppermute | solution.py:358
  4.8 25.3 %collective-permute-start.14 = (bf16[160,512]{1,0:T(8,128)(2,1)S(1)}, bf16[160,512]{1,0:T(8,128)(2,1)S(1)}, u32[]{:S(2)}, u32[]{:S(2)}) collective-permute-start(bf16[160,512]{1,0:T(8,128)(2,1)S(1)} %constant_dynamic-slice_fusion), channel_id=1, source_target_pairs={{0,16},{8,24},{16,0},{24,8},{1,17},{9,25},{17,1},{25,9},{2,18},{10... | collective-permute-start | bytes 491528 | tf_op jit(solution)/shard_map/ppermute | solution.py:358
  9.2 1.7 %copy-start.24 = (s32[8]{0:T(128)S(1)}, s32[8]{0:T(128)}, u32[]{:S(2)}) copy-start(s32[8]{0:T(128)} %param.20) | copy-start | bytes 100
  9.2 2.1 %copy-start.11 = (s32[8]{0:T(128)S(1)}, s32[8]{0:T(128)}, u32[]{:S(2)}) copy-start(s32[8]{0:T(128)} %param.19) | copy-start | bytes 100
  9.2 2.0 %copy-start.12 = (f32[8]{0:T(128)S(1)}, f32[8]{0:T(128)}, u32[]{:S(2)}) copy-start(f32[8]{0:T(128)} %param.18) | copy-start | bytes 100
  9.2 3.1 %copy-start.13 = (f32[128]{0:T(128)S(1)}, f32[128]{0:T(128)}, u32[]{:S(2)}) copy-start(f32[128]{0:T(128)} %param.16) | copy-start | bytes 1540
  9.2 3.1 %copy-start.14 = (f32[128]{0:T(128)S(1)}, f32[128]{0:T(128)}, u32[]{:S(2)}) copy-start(f32[128]{0:T(128)} %param.17) | copy-start | bytes 1540
  9.3 16.1 %collective-permute-start.20 = (bf16[4,2,2,160,128]{4,3,2,1,0:T(8,128)(2,1)S(1)}, bf16[4,2,2,160,128]{4,3,2,1,0:T(8,128)(2,1)}, u32[]{:S(2)}, u32[]{:S(2)}) collective-permute-start(bf16[4,2,2,160,128]{4,3,2,1,0:T(8,128)(2,1)S(1)} %dynamic-slice_bitcast_fusion), channel_id=1, source_target_pairs={{0,2},{2,0},{1,3},{3,1},{4,6},{6,4},{5,7},{7,5},{8,10},{10,8},{9,1... | collective-permute-start | bytes 1966088 | tf_op jit(solution)/shard_map/ppermute | solution.py:358
  12.4 14.3 %collective-permute-start.2 = (f32[128]{0:T(128)S(1)}, f32[128]{0:T(128)S(1)}, u32[]{:S(2)}, u32[]{:S(2)}) collective-permute-start(f32[128]{0:T(128)S(1)} %and_select_fusion), channel_id=1, source_target_pairs={{0,4},{4,0},{1,5},{5,1},{2,6},{6,2},{3,7},{7,3},{8,12},{12,8},{9,1... | collective-permute-start | bytes 1544 | tf_op jit(solution)/shard_map/ppermute | solution.py:358
  17.2 10.9 %collective-permute-start.3 = (bf16[128,256]{1,0:T(8,128)(2,1)}, bf16[128,256]{1,0:T(8,128)(2,1)S(1)}, u32[]{:S(2)}, u32[]{:S(2)}) collective-permute-start(bf16[128,256]{1,0:T(8,128)(2,1)} %get-tuple-element.23), channel_id=1, source_target_pairs={{0,4},{4,0},{1,5},{5,1},{2,6},{6,2},{3,7},{7,3},{8,12},{12,8},{9,1... | collective-permute-start | bytes 196616 | tf_op jit(solution)/shard_map/ppermute | solution.py:358
  17.8 8.9 %copy-start.9 = (bf16[128,256]{1,0:T(8,128)(2,1)S(1)}, bf16[128,256]{1,0:T(8,128)(2,1)}, u32[]{:S(2)}) copy-start(bf16[128,256]{1,0:T(8,128)(2,1)} %get-tuple-element.22) | copy-start | bytes 196612
  17.8 11.8 %copy-start.15 = (bf16[128,1280]{1,0:T(8,128)(2,1)S(1)}, bf16[128,1280]{1,0:T(8,128)(2,1)}, u32[]{:S(2)}) copy-start(bf16[128,1280]{1,0:T(8,128)(2,1)} %get-tuple-element.21) | copy-start | bytes 983044
  26.6 29.3 %collective-permute-start.21 = (bf16[2,4,2,160,128]{4,3,2,1,0:T(8,128)(2,1)S(1)}, bf16[2,4,2,160,128]{4,3,2,1,0:T(8,128)(2,1)}, u32[]{:S(2)}, u32[]{:S(2)}) collective-permute-start(bf16[2,4,2,160,128]{4,3,2,1,0:T(8,128)(2,1)S(1)} %pad_maximum_fusion.1), channel_id=1, source_target_pairs={{0,1},{1,0},{2,3},{3,2},{4,5},{5,4},{6,7},{7,6},{8,9},{9,8},{10,11... | collective-permute-start | bytes 1966088 | tf_op jit(solution)/shard_map/ppermute | solution.py:358
  26.7 6.6 %collective-permute-start.15 = (bf16[160,512]{1,0:T(8,128)(2,1)S(1)}, bf16[160,512]{1,0:T(8,128)(2,1)S(1)}, u32[]{:S(2)}, u32[]{:S(2)}) collective-permute-start(bf16[160,512]{1,0:T(8,128)(2,1)S(1)} %constant_dynamic-slice_fusion), channel_id=1, source_target_pairs={{0,24},{8,0},{16,8},{24,16},{1,25},{9,1},{17,9},{25,17},{2,26},{10... | collective-permute-start | bytes 491528 | tf_op jit(solution)/shard_map/ppermute | solution.py:358
  28.1 16.8 %collective-permute-start = (bf16[128,1280]{1,0:T(8,128)(2,1)}, bf16[128,1280]{1,0:T(8,128)(2,1)S(1)}, u32[]{:S(2)}, u32[]{:S(2)}) collective-permute-start(bf16[128,1280]{1,0:T(8,128)(2,1)} %get-tuple-element.20), channel_id=1, source_target_pairs={{0,4},{4,0},{1,5},{5,1},{2,6},{6,2},{3,7},{7,3},{8,12},{12,8},{9,1... | collective-permute-start | bytes 983048 | tf_op jit(solution)/shard_map/ppermute | solution.py:358
  29.6 15.7 %collective-permute-start.1 = (bf16[128,1280]{1,0:T(8,128)(2,1)S(1)}, bf16[128,1280]{1,0:T(8,128)(2,1)}, u32[]{:S(2)}, u32[]{:S(2)}) collective-permute-start(bf16[128,1280]{1,0:T(8,128)(2,1)S(1)} %copy-done.15), channel_id=1, source_target_pairs={{0,4},{4,0},{1,5},{5,1},{2,6},{6,2},{3,7},{7,3},{8,12},{12,8},{9,1... | collective-permute-start | bytes 983048 | tf_op jit(solution)/shard_map/ppermute | solution.py:358
  30.2 15.1 %copy-start.10 = (bf16[256,256]{1,0:T(8,128)(2,1)}, bf16[256,256]{1,0:T(8,128)(2,1)S(1)}, u32[]{:S(2)}) copy-start(bf16[256,256]{1,0:T(8,128)(2,1)S(1)} %constant_dynamic-update-slice_fusion.refs_0_) | copy-start | bytes 393220
  30.2 6.1 %collective-permute-start.4 = (bf16[256,256]{1,0:T(8,128)(2,1)S(1)}, bf16[256,256]{1,0:T(8,128)(2,1)S(1)}, u32[]{:S(2)}, u32[]{:S(2)}) collective-permute-start(bf16[256,256]{1,0:T(8,128)(2,1)S(1)} %constant_dynamic-update-slice_fusion.refs_0_), channel_id=1, source_target_pairs={{0,8},{8,16},{16,24},{1,9},{9,17},{17,25},{2,10},{10,18},{18,26},{... | collective-permute-start | bytes 393224 | tf_op jit(solution)/shard_map/ppermute | solution.py:358
  33.4 11.5 %collective-permute-start.5 = (bf16[256,256]{1,0:T(8,128)(2,1)S(1)}, bf16[256,256]{1,0:T(8,128)(2,1)}, u32[]{:S(2)}, u32[]{:S(2)}) collective-permute-start(bf16[256,256]{1,0:T(8,128)(2,1)S(1)} %constant_dynamic-update-slice_fusion.refs_0_), channel_id=1, source_target_pairs={{0,16},{8,24},{1,17},{9,25},{2,18},{10,26},{3,19},{11,27},{4,20},{... | collective-permute-start | bytes 393224 | tf_op jit(solution)/shard_map/ppermute | solution.py:358
  36.9 8.0 %collective-permute-start.6 = (bf16[256,256]{1,0:T(8,128)(2,1)S(1)}, bf16[256,256]{1,0:T(8,128)(2,1)}, u32[]{:S(2)}, u32[]{:S(2)}) collective-permute-start(bf16[256,256]{1,0:T(8,128)(2,1)S(1)} %constant_dynamic-update-slice_fusion.refs_0_), channel_id=1, source_target_pairs={{0,24},{1,25},{2,26},{3,27},{4,28},{5,29},{6,30},{7,31}} | collective-permute-start | bytes 393224 | tf_op jit(solution)/shard_map/ppermute | solution.py:358
  44.9 37.3 %collective-permute-start.16 = (bf16[4,160,512]{2,1,0:T(8,128)(2,1)}, bf16[4,160,512]{2,1,0:T(8,128)(2,1)}, u32[]{:S(2)}, u32[]{:S(2)}) collective-permute-start(bf16[4,160,512]{2,1,0:T(8,128)(2,1)} %pad_maximum_fusion.refs_4_), channel_id=1, source_target_pairs={{0,1},{1,0},{2,3},{3,2},{4,5},{5,4},{6,7},{7,6},{8,9},{9,8},{10,11... | collective-permute-start | bytes 1966088 | tf_op jit(solution)/shard_map/ppermute | solution.py:358
  52.0 9.8 %collective-permute-start.7 = (bf16[256,256]{1,0:T(8,128)(2,1)}, bf16[256,256]{1,0:T(8,128)(2,1)S(1)}, u32[]{:S(2)}, u32[]{:S(2)}) collective-permute-start(bf16[256,256]{1,0:T(8,128)(2,1)} %get-tuple-element.25), channel_id=1, source_target_pairs={{8,0},{16,8},{24,16},{9,1},{17,9},{25,17},{10,2},{18,10},{26,18},{... | collective-permute-start | bytes 393224 | tf_op jit(solution)/shard_map/ppermute | solution.py:358
  53.3 14.6 %collective-permute-start.8 = (bf16[256,256]{1,0:T(8,128)(2,1)}, bf16[256,256]{1,0:T(8,128)(2,1)S(1)}, u32[]{:S(2)}, u32[]{:S(2)}) collective-permute-start(bf16[256,256]{1,0:T(8,128)(2,1)} %get-tuple-element.26), channel_id=1, source_target_pairs={{16,0},{24,8},{17,1},{25,9},{18,2},{26,10},{19,3},{27,11},{20,4},{... | collective-permute-start | bytes 393224 | tf_op jit(solution)/shard_map/ppermute | solution.py:358
  54.6 13.3 %collective-permute-start.9 = (bf16[256,256]{1,0:T(8,128)(2,1)}, bf16[256,256]{1,0:T(8,128)(2,1)S(1)}, u32[]{:S(2)}, u32[]{:S(2)}) collective-permute-start(bf16[256,256]{1,0:T(8,128)(2,1)} %get-tuple-element.27), channel_id=1, source_target_pairs={{24,0},{25,1},{26,2},{27,3},{28,4},{29,5},{30,6},{31,7}} | collective-permute-start | bytes 393224 | tf_op jit(solution)/shard_map/ppermute | solution.py:358
  55.9 11.9 %copy-start.8 = (bf16[256,256]{1,0:T(8,128)(2,1)S(1)}, bf16[256,256]{1,0:T(8,128)(2,1)}, u32[]{:S(2)}) copy-start(bf16[256,256]{1,0:T(8,128)(2,1)} %get-tuple-element.24) | copy-start | bytes 393220
  57.2 36.0 %collective-permute-start.22 = (bf16[2,2,4,160,128]{4,3,2,1,0:T(8,128)(2,1)S(1)}, bf16[2,2,4,160,128]{4,3,2,1,0:T(8,128)(2,1)}, u32[]{:S(2)}, u32[]{:S(2)}) collective-permute-start(bf16[2,2,4,160,128]{4,3,2,1,0:T(8,128)(2,1)S(1)} %pad_maximum_fusion.3), channel_id=1, source_target_pairs={{0,4},{4,0},{1,5},{5,1},{2,6},{6,2},{3,7},{7,3},{8,12},{12,8},{9,1... | collective-permute-start | bytes 1966088 | tf_op jit(solution)/shard_map/ppermute | solution.py:358
  67.9 14.3 %copy-start.7 = (bf16[256,256]{1,0:T(8,128)(2,1)}, bf16[256,256]{1,0:T(8,128)(2,1)S(1)}, u32[]{:S(2)}) copy-start(bf16[256,256]{1,0:T(8,128)(2,1)S(1)} %add_convert_fusion.refs_0_) | copy-start | bytes 393220
  67.9 9.3 %collective-permute-start.11 = (bf16[256,256]{1,0:T(8,128)(2,1)S(1)}, bf16[256,256]{1,0:T(8,128)(2,1)S(1)}, u32[]{:S(2)}, u32[]{:S(2)}) collective-permute-start(bf16[256,256]{1,0:T(8,128)(2,1)S(1)} %add_convert_fusion.refs_0_), channel_id=1, source_target_pairs={{0,4},{4,0},{1,5},{5,1},{2,6},{6,2},{3,7},{7,3},{8,12},{12,8},{9,1... | collective-permute-start | bytes 393224 | tf_op jit(solution)/shard_map/ppermute | solution.py:358
  69.5 9.3 %collective-permute-start.10 = (bf16[256,256]{1,0:T(8,128)(2,1)S(1)}, bf16[256,256]{1,0:T(8,128)(2,1)S(1)}, u32[]{:S(2)}, u32[]{:S(2)}) collective-permute-start(bf16[256,256]{1,0:T(8,128)(2,1)S(1)} %add_convert_fusion.refs_0_), channel_id=1, source_target_pairs={{0,2},{2,0},{1,3},{3,1},{4,6},{6,4},{5,7},{7,5},{8,10},{10,8},{9,1... | collective-permute-start | bytes 393224 | tf_op jit(solution)/shard_map/ppermute | solution.py:358
  77.2 5.0 %copy-start.17 = (bf16[256,256]{1,0:T(8,128)(2,1)}, bf16[256,256]{1,0:T(8,128)(2,1)S(1)}, u32[]{:S(2)}) copy-start(bf16[256,256]{1,0:T(8,128)(2,1)S(1)} %collective-permute-done.11.refs_2_.refs_4_) | copy-start | bytes 393220
  77.2 5.0 %collective-permute-start.12 = (bf16[256,256]{1,0:T(8,128)(2,1)S(1)}, bf16[256,256]{1,0:T(8,128)(2,1)S(1)}, u32[]{:S(2)}, u32[]{:S(2)}) collective-permute-start(bf16[256,256]{1,0:T(8,128)(2,1)S(1)} %collective-permute-done.11.refs_2_.refs_4_), channel_id=1, source_target_pairs={{0,2},{2,0},{1,3},{3,1},{4,6},{6,4},{5,7},{7,5},{8,10},{10,8},{9,1... | collective-permute-start | bytes 393224 | tf_op jit(solution)/shard_map/ppermute | solution.py:358
  78.7 3.5 %copy-start.18 = (bf16[256,256]{1,0:T(8,128)(2,1)}, bf16[256,256]{1,0:T(8,128)(2,1)S(1)}, u32[]{:S(2)}) copy-start(bf16[256,256]{1,0:T(8,128)(2,1)S(1)} %collective-permute-done.10.refs_1_) | copy-start | bytes 393220
  87.1 14.9 %collective-permute-start.17 = (bf16[128,1280]{1,0:T(8,128)(2,1)}, bf16[128,1280]{1,0:T(8,128)(2,1)S(1)}, u32[]{:S(2)}, u32[]{:S(2)}) collective-permute-start(bf16[128,1280]{1,0:T(8,128)(2,1)} %get-tuple-element.29), channel_id=1, source_target_pairs={{0,2},{2,0},{1,3},{3,1},{4,6},{6,4},{5,7},{7,5},{8,10},{10,8},{9,1... | collective-permute-start | bytes 983048 | tf_op jit(solution)/shard_map/ppermute | solution.py:358
  88.6 1.6 %collective-permute-start.23 = (bf16[256,256]{1,0:T(8,128)(2,1)}, bf16[256,256]{1,0:T(8,128)(2,1)S(1)}, u32[]{:S(2)}, u32[]{:S(2)}) collective-permute-start(bf16[256,256]{1,0:T(8,128)(2,1)} %copy-done.7), channel_id=1, source_target_pairs={{0,1},{1,0},{2,3},{3,2},{4,5},{5,4},{6,7},{7,6},{8,9},{9,8},{10,11... | collective-permute-start | bytes 393224 | tf_op jit(solution)/shard_map/ppermute | solution.py:358
  88.6 1.7 %collective-permute-start.24 = (bf16[256,256]{1,0:T(8,128)(2,1)}, bf16[256,256]{1,0:T(8,128)(2,1)S(1)}, u32[]{:S(2)}, u32[]{:S(2)}) collective-permute-start(bf16[256,256]{1,0:T(8,128)(2,1)} %copy-done.18), channel_id=1, source_target_pairs={{0,1},{1,0},{2,3},{3,2},{4,5},{5,4},{6,7},{7,6},{8,9},{9,8},{10,11... | collective-permute-start | bytes 393224 | tf_op jit(solution)/shard_map/ppermute | solution.py:358
  89.1 2.7 %collective-permute-start.25 = (bf16[256,256]{1,0:T(8,128)(2,1)}, bf16[256,256]{1,0:T(8,128)(2,1)S(1)}, u32[]{:S(2)}, u32[]{:S(2)}) collective-permute-start(bf16[256,256]{1,0:T(8,128)(2,1)} %copy-done.17), channel_id=1, source_target_pairs={{0,1},{1,0},{2,3},{3,2},{4,5},{5,4},{6,7},{7,6},{8,9},{9,8},{10,11... | collective-permute-start | bytes 393224 | tf_op jit(solution)/shard_map/ppermute | solution.py:358
  90.2 3.1 %copy-start.21 = (bf16[256,256]{1,0:T(8,128)(2,1)}, bf16[256,256]{1,0:T(8,128)(2,1)S(1)}, u32[]{:S(2)}) copy-start(bf16[256,256]{1,0:T(8,128)(2,1)S(1)} %collective-permute-done.23.refs_2_) | copy-start | bytes 393220
  90.2 3.1 %collective-permute-start.26 = (bf16[256,256]{1,0:T(8,128)(2,1)}, bf16[256,256]{1,0:T(8,128)(2,1)}, u32[]{:S(2)}, u32[]{:S(2)}) collective-permute-start(bf16[256,256]{1,0:T(8,128)(2,1)} %copy-done.19), channel_id=1, source_target_pairs={{0,1},{1,0},{2,3},{3,2},{4,5},{5,4},{6,7},{7,6},{8,9},{9,8},{10,11... | collective-permute-start | bytes 393224 | tf_op jit(solution)/shard_map/ppermute | solution.py:358
  90.3 2.9 %copy-start.22 = (bf16[256,256]{1,0:T(8,128)(2,1)}, bf16[256,256]{1,0:T(8,128)(2,1)S(1)}, u32[]{:S(2)}) copy-start(bf16[256,256]{1,0:T(8,128)(2,1)S(1)} %collective-permute-done.24.refs_3_) | copy-start | bytes 393220
  90.3 11.6 %collective-permute-start.18 = (bf16[128,1280]{1,0:T(8,128)(2,1)}, bf16[128,1280]{1,0:T(8,128)(2,1)S(1)}, u32[]{:S(2)}, u32[]{:S(2)}) collective-permute-start(bf16[128,1280]{1,0:T(8,128)(2,1)} %get-tuple-element.30), channel_id=1, source_target_pairs={{0,4},{4,0},{1,5},{5,1},{2,6},{6,2},{3,7},{7,3},{8,12},{12,8},{9,1... | collective-permute-start | bytes 983048 | tf_op jit(solution)/shard_map/ppermute | solution.py:358
  91.9 15.6 %collective-permute-start.19 = (bf16[128,1280]{1,0:T(8,128)(2,1)}, bf16[128,1280]{1,0:T(8,128)(2,1)S(1)}, u32[]{:S(2)}, u32[]{:S(2)}) collective-permute-start(bf16[128,1280]{1,0:T(8,128)(2,1)} %get-tuple-element.31), channel_id=1, source_target_pairs={{0,6},{2,4},{4,2},{6,0},{1,7},{3,5},{5,3},{7,1},{8,14},{10,12},{12... | collective-permute-start | bytes 983048 | tf_op jit(solution)/shard_map/ppermute | solution.py:476
  96.4 14.5 %collective-permute-start.27 = (bf16[160,512]{1,0:T(8,128)(2,1)}, bf16[160,512]{1,0:T(8,128)(2,1)S(1)}, u32[]{:S(2)}, u32[]{:S(2)}) collective-permute-start(bf16[160,512]{1,0:T(8,128)(2,1)} %get-tuple-element.33), channel_id=1, source_target_pairs={{0,8},{8,16},{16,24},{24,0},{1,9},{9,17},{17,25},{25,1},{2,10},{10... | collective-permute-start | bytes 491528 | tf_op jit(solution)/shard_map/ppermute | solution.py:358
  98.1 14.8 %collective-permute-start.28 = (bf16[160,512]{1,0:T(8,128)(2,1)}, bf16[160,512]{1,0:T(8,128)(2,1)S(1)}, u32[]{:S(2)}, u32[]{:S(2)}) collective-permute-start(bf16[160,512]{1,0:T(8,128)(2,1)} %get-tuple-element.34), channel_id=1, source_target_pairs={{0,16},{8,24},{16,0},{24,8},{1,17},{9,25},{17,1},{25,9},{2,18},{10... | collective-permute-start | bytes 491528 | tf_op jit(solution)/shard_map/ppermute | solution.py:358
  102.0 5.5 %copy-start.2 = (bf16[128,1280]{1,0:T(8,128)(2,1)}, bf16[128,1280]{1,0:T(8,128)(2,1)S(1)}, u32[]{:S(2)}) copy-start(bf16[128,1280]{1,0:T(8,128)(2,1)S(1)} %collective-permute-done.17.refs_1_) | copy-start | bytes 983044
  102.0 10.9 %collective-permute-start.29 = (bf16[160,512]{1,0:T(8,128)(2,1)}, bf16[160,512]{1,0:T(8,128)(2,1)S(1)}, u32[]{:S(2)}, u32[]{:S(2)}) collective-permute-start(bf16[160,512]{1,0:T(8,128)(2,1)} %get-tuple-element.35), channel_id=1, source_target_pairs={{0,24},{8,0},{16,8},{24,16},{1,25},{9,1},{17,9},{25,17},{2,26},{10... | collective-permute-start | bytes 491528 | tf_op jit(solution)/shard_map/ppermute | solution.py:358
  102.0 5.5 %copy-start.3 = (bf16[128,1280]{1,0:T(8,128)(2,1)}, bf16[128,1280]{1,0:T(8,128)(2,1)S(1)}, u32[]{:S(2)}) copy-start(bf16[128,1280]{1,0:T(8,128)(2,1)S(1)} %collective-permute-done.18.refs_2_) | copy-start | bytes 983044
  108.2 4.7 %copy-start.6 = (bf16[160,512]{1,0:T(8,128)(2,1)S(1)}, bf16[160,512]{1,0:T(8,128)(2,1)}, u32[]{:S(2)}) copy-start(bf16[160,512]{1,0:T(8,128)(2,1)} %get-tuple-element.32) | copy-start | bytes 491524
  110.9 2.1 %copy-start.1 = (bf16[160,512]{1,0:T(8,128)(2,1)S(1)}, bf16[160,512]{1,0:T(8,128)(2,1)}, u32[]{:S(2)}) copy-start(bf16[160,512]{1,0:T(8,128)(2,1)} %param.23) | copy-start | bytes 491524
  (7 other events, 6.1 us)
where the time goes:
time: 125 us; the launch traced here: 123 us
  starting transfers between devices  43.7 us (35%)
  waiting for transfers between devices  35.9 us (29%)
  Pallas kernels  19 us (15%)
  local copies, waits for them, and re-layouts  10.6 us (8%)
  blocking collectives  7.9 us (6%)
  other arithmetic  5.31 us (4%)
    ppermute x29, starting transfers between devices, shift(): return lax.ppermute(value, axis, pairs)  43.2 us
    ppermute x29, waiting for transfers between devices, shift(): return lax.ppermute(value, axis, pairs)  30.4 us
    all_gather x1, blocking collectives, step(): new_proj = lax.all_gather(new_rows, ('y', 'core'), axis=0, tiled=True)  7.9 us
    pallas_call x1, Pallas kernels, attention_parts(): pl.pallas_call(functools.partial(attention_kernel, slots, half), grid_spe...  6.31 us
    unnamed x53, local copies, waits for them, and re-layouts  6.17 us
    ppermute x1, waiting for transfers between devices, step(): found[y_size + k] = lax.ppermute(products[y_size + k], ('x', 'y'), pairs)  5.47 us
    pallas_call x1, Pallas kernels, row_products(): pl.pallas_call(functools.partial(row_kernel, z_size, y_size), in_specs=[p...  4.2 us
    pallas_call x1, Pallas kernels, owner_products(): pl.pallas_call(functools.partial(owner_kernel, z_size, pieces), in_specs=...  3.13 us
  transfers between devices with their start and end apart: 30, of which 10 were waited for; matrix products, arithmetic and copies ran while one was open for 8% of the time, Pallas kernels for 15%

commit v1 on v0

--- a/solution.py
+++ b/solution.py
@@ -25,6 +25,8 @@
 bias_first = 1.0 - 0.9**10
 bias_second = 1.0 - 0.95**10
 
+ROOM = pltpu.CompilerParams(vmem_limit_bytes=16 * 2**20)
+
 
 def advantages(rewards, group_ids):
     same = (group_ids[:, None] == group_ids[None, :]).astype(jnp.float32)
@@ -62,13 +64,11 @@
             [key_refs[n][part, :] for n in range(slots) for part in (rows, far_rows)], axis=0
         )
         grads = []
+        coeff = jnp.concatenate([c_own[roll : roll + 1, :], c_far[roll : roll + 1, :]], axis=1)
         for head in range(per_group):
             cols = slice(head * HEAD, (head + 1) * HEAD)
             query = jnp.concatenate([q_own[rows, cols], q_far[rows, cols]], axis=0)
-            grads += [
-                (c[rows, :] * g[rows, cols].astype(jnp.float32)).astype(jnp.bfloat16)
-                for c, g in ((c_own, g_own), (c_far, g_far))
-            ]
+            grads += [g_own[rows, cols], g_far[rows, cols]]
             scores = (
                 lax.dot_general(
                     keys, query, (((1,), (1,)), ((), ())), preferred_element_type=jnp.float32
@@ -85,10 +85,10 @@
             )
             expo = [jnp.exp(piece - top) for piece in pieces]
             total = sum(jnp.sum(piece, axis=0, keepdims=True) for piece in expo)
-            inverse = 1.0 / total
+            weight = coeff / total
             for n in range(slots):
                 probs[n * block : (n + 1) * block, head * block : (head + 1) * block] = (
-                    expo[n] * inverse
+                    expo[n] * weight
                 ).astype(jnp.bfloat16)
         summed = jnp.dot(
             probs[...], jnp.concatenate(grads, axis=0), preferred_element_type=jnp.float32
@@ -106,7 +106,7 @@
     half = tok_rows // ROLLS
     own_spec = pl.BlockSpec((tok_rows, per_head), lambda h, place: (0, place[1] * kv_heads + h))
     far_spec = pl.BlockSpec((tok_rows, per_head), lambda h, place: (0, h))
-    coeff_spec = pl.BlockSpec((tok_rows, 1), lambda h, place: (0, 0))
+    coeff_spec = pl.BlockSpec(c_own.shape, lambda h, place: (0, 0))
     k_spec = pl.BlockSpec((PAIR * tok_rows, HEAD), lambda h, place: (0, h))
     shape = jax.ShapeDtypeStruct(key_blocks[0].shape, jnp.bfloat16)
     work = 4 * kv_heads * per_head * ROLLS * (PAIR * half) ** 2 * slots
@@ -124,6 +124,7 @@
             ],
         ),
         out_shape=[shape] * slots,
+        compiler_params=ROOM,
         cost_estimate=pl.CostEstimate(
             flops=work, bytes_accessed=8 * tok_rows * q_cols, transcendentals=work // 256
         ),
@@ -161,80 +162,190 @@
                 for cols in (HEAD, HEAD, q_cols, q_cols)
             ],
         ),
-        out_shape=[half(HEAD), half(HEAD), half(q_cols), half(q_cols)],
+        out_shape=[
+            jax.ShapeDtypeStruct((PAIR * tok_rows, steps * HEAD), jnp.bfloat16),
+            half(HEAD),
+            half(q_cols),
+            half(q_cols),
+        ],
         cost_estimate=pl.CostEstimate(
             flops=0, bytes_accessed=8 * tok_rows * steps * q_cols, transcendentals=0
         ),
     )(place, key_vectors, key_vectors, queries, logp_grad)
 
 
-def owner_kernel(z_size, pieces, place, near, far, *refs):
-    values, outs = refs[: 2 * pieces], refs[2 * pieces :]
-    sources = [(c, y) for c in range(near.shape[0]) for y in range(near.shape[1])]
-    first = jnp.concatenate([ref[...] for ref in values[:pieces]], axis=0)
-    second = jnp.concatenate([ref[...] for ref in values[pieces:]], axis=0)
-    half = first.shape[1]
-    for k in range(z_size):
-        owner = place[0] + k
-        owner = jnp.where(owner >= z_size, owner - z_size, owner)
-        near_cols = [near[c, y, owner] for c, y in sources]
-        far_cols = [far[c, y, owner] for c, y in sources]
-        own_first = [cols for pair in zip(near_cols, far_cols) for cols in pair]
-        far_first = [cols for pair in zip(far_cols, near_cols) for cols in pair]
-        outs[k][:, :half] = jnp.dot(
-            jnp.concatenate(own_first, axis=1), first, preferred_element_type=jnp.float32
-        ).astype(jnp.bfloat16)
-        outs[k][:, half:] = jnp.dot(
-            jnp.concatenate(far_first, axis=1), second, preferred_element_type=jnp.float32
-        ).astype(jnp.bfloat16)
+def owner_kernel(pieces, z_size, place, near, far, *refs):
+    values, outs = refs[: 2 * pieces], refs[2 * pieces : 2 * pieces + z_size]
+    token_rows = refs[2 * pieces + z_size]
+    buffers, totals, sems = refs[-3:]
+    copies = [
+        pltpu.make_async_copy(source, buffers.at[n], sems.at[n])
+        for n, source in enumerate((near, far))
+    ]
+    for copy in copies:
+        copy.start()
+    sides = near.shape[0] // PAIR
+    rows, tokens = near.shape[2:]
+    half = values[0].shape[1]
+    for n, copy in enumerate(copies):
+        copy.wait()
+        for m in range(PAIR):
+            columns = jnp.concatenate(
+                [
+                    buffers[n, (x + m) % PAIR * sides + y].reshape(z_size * rows, tokens)
+                    for y in range(sides)
+                    for x in range(PAIR)
+                ],
+                axis=1,
+            )
+            blocks = values[m * pieces + n * sides : m * pieces + (n + 1) * sides]
+            product = jnp.dot(
+                columns,
+                jnp.concatenate([ref[...] for ref in blocks], axis=0),
+                preferred_element_type=jnp.float32,
+            )
+            part = slice(m * half, (m + 1) * half)
+            totals[:, part] = product if n == 0 else totals[:, part] + product
+    flag = place[1] == 0
+    for x in range(PAIR):
+        for y in range(sides):
+            low = values[y][x * tokens : (x + 1) * tokens, :]
+            high = values[pieces + y][(1 - x) * tokens : (2 - x) * tokens, :]
+            at = (x * sides + y) * tokens
+            token_rows[at : at + tokens, :half] = jnp.where(flag, low, high)
+            token_rows[at : at + tokens, half:] = jnp.where(flag, high, low)
+    for k, out in enumerate(outs):
+        at = place[0] + k
+        start = pl.multiple_of(jnp.where(at >= z_size, at - z_size, at) * rows, rows)
+        out[...] = totals[pl.ds(start, rows), :].astype(jnp.bfloat16)
+
+
+def plain_owner_products(place, near, far, first, second):
+    z_size, rows, tokens = near.shape[1:]
+    sides = near.shape[0] // PAIR
+    halves = []
+    for m, blocks in enumerate((first, second)):
+        total = 0.0
+        for n, array in enumerate((near, far)):
+            order = [(x + m) % PAIR * sides + y for y in range(sides) for x in range(PAIR)]
+            columns = jnp.stack([array[at] for at in order], axis=2)
+            total = total + jnp.dot(
+                columns.reshape(z_size * rows, -1),
+                jnp.concatenate(blocks[n * sides : (n + 1) * sides], axis=0),
+                preferred_element_type=jnp.float32,
+            )
+        halves.append(total.astype(jnp.bfloat16))
+    every = jnp.concatenate(halves, axis=1).reshape(z_size, rows, -1)
+    groups = []
+    for x in range(PAIR):
+        for y in range(sides):
+            low = first[y][x * tokens : (x + 1) * tokens]
+            high = second[y][(1 - x) * tokens : (2 - x) * tokens]
+            groups.append(
+                jnp.where(
+                    place[1] == 0,
+                    jnp.concatenate([low, high], axis=1),
+                    jnp.concatenate([high, low], axis=1),
+                )
+            )
+    return [cut(every, turned(place[0], k, z_size), 0) for k in range(z_size)] + [
+        jnp.concatenate(groups, axis=0)
+    ]
 
 
 def owner_products(place, near, far, first, second):
-    _, _, z_size, rows, _ = near.shape
+    z_size, rows, tokens = near.shape[1:]
+    if rows % 16:
+        return plain_owner_products(place, near, far, first, second)
     pieces = len(first)
     width = 2 * first[0].shape[1]
+    whole = pl.BlockSpec(memory_space=pltpu.VMEM)
     shape = jax.ShapeDtypeStruct((rows, width), jnp.bfloat16)
+    return pl.pallas_call(
+        functools.partial(owner_kernel, pieces, z_size),
+        in_specs=[pl.BlockSpec(memory_space=pltpu.SMEM)]
+        + [pl.BlockSpec(memory_space=pl.ANY)] * 2
+        + [whole] * (2 * pieces),
+        out_specs=[whole] * (z_size + 1),
+        out_shape=[shape] * z_size
+        + [jax.ShapeDtypeStruct((near.shape[0] * tokens, width), jnp.bfloat16)],
+        scratch_shapes=[
+            pltpu.VMEM((2, *near.shape), jnp.bfloat16),
+            pltpu.VMEM((z_size * rows, width), jnp.float32),
+            pltpu.SemaphoreType.DMA((2,)),
+        ],
+        compiler_params=ROOM,
+        cost_estimate=pl.CostEstimate(
+            flops=4 * near.size * width, bytes_accessed=8 * near.size, transcendentals=0
+        ),
+    )(place, near, far, *first, *second)
+
+
+def row_kernel(z_size, groups, place, token_rows, *refs):
+    proj, outs = refs[:4], refs[4 : 4 + groups]
+    rows_all, sems = refs[-2:]
+    rows, tok_rows = proj[0].shape[1], outs[0].shape[0]
+    copies = []
+    for k, bits in enumerate(flips(z_size)):
+        for c in range(2):
+            at_core = place[3] if c == 0 else 1 - place[3]
+            start = ((place[0] ^ bits) * 2 + at_core) * rows
+            group, at = divmod(k, z_size // 2)
+            copies.append(
+                pltpu.make_async_copy(
+                    proj[2 * c + group].at[at],
+                    rows_all.at[pl.ds(pl.multiple_of(start, rows), rows), :],
+                    sems.at[2 * k + c],
+                )
+            )
+    for copy in copies:
+        copy.start()
+    for copy in copies:
+        copy.wait()
+    product = lax.dot_general(
+        token_rows[...],
+        rows_all[...],
+        (((1,), (1,)), ((), ())),
+        preferred_element_type=jnp.float32,
+    ).astype(jnp.bfloat16)
+    for n, out in enumerate(outs):
+        out[...] = product[n * tok_rows : (n + 1) * tok_rows]
+
+
+def plane_kernel(place, columns, *outs):
+    y_size = columns.shape[2]
+    for x in range(PAIR):
+        for y in range(y_size):
+            at_x, at_y = place[1] + x, place[2] + y
+            at_x = jnp.where(at_x >= PAIR, at_x - PAIR, at_x)
+            at_y = jnp.where(at_y >= y_size, at_y - y_size, at_y)
+            out = outs[x * y_size + y]
+            for z in range(columns.shape[0]):
+                out[z] = columns[z, at_x, at_y]
+
+
+def core_kernel(place, *refs):
+    pieces, (near, far) = refs[:-2], refs[-2:]
+    for n, piece in enumerate(pieces):
+        for z in range(piece.shape[0]):
+            near[n, z] = piece[z, place[3]]
+            far[n, z] = piece[z, 1 - place[3]]
+
+
+def sliced(kernel, place, arrays, shapes):
     whole = pl.BlockSpec(memory_space=pltpu.VMEM)
     return pl.pallas_call(
-        functools.partial(owner_kernel, z_size, pieces),
-        in_specs=[pl.BlockSpec(memory_space=pltpu.SMEM)] + [whole] * (2 + 2 * pieces),
-        out_specs=[whole] * z_size,
-        out_shape=[shape] * z_size,
+        kernel,
+        in_specs=[pl.BlockSpec(memory_space=pltpu.SMEM)] + [whole] * len(arrays),
+        out_specs=[whole] * len(shapes),
+        out_shape=[jax.ShapeDtypeStruct(shape, jnp.bfloat16) for shape in shapes],
+        compiler_params=ROOM,
         cost_estimate=pl.CostEstimate(
-            flops=4 * near.size * width, bytes_accessed=8 * near.size, transcendentals=0
-        ),
-    )(place, near, far, *first, *second)
-
-
-def row_kernel(z_size, y_size, place, *refs):
-    ends = 2 * y_size, len(refs) - 1 - 2 * y_size
-    values, proj, outs = refs[: ends[0]], refs[ends[0] : ends[1]], refs[ends[1] : -1]
-    rows_all = refs[-1]
-    rows, tok_rows = proj[0].shape[1], outs[0].shape[0]
-    for c, ref in enumerate(proj):
-        at_core = place[3] - c
-        at_core = jnp.where(at_core < 0, at_core + len(proj), at_core)
-        for k in range(z_size):
-            at_z = place[0] - k
-            at_z = jnp.where(at_z < 0, at_z + z_size, at_z)
-            start = pl.multiple_of((at_z * len(proj) + at_core) * rows, rows)
-            rows_all[pl.ds(start, rows), :] = ref[k]
-    for y in range(y_size):
-        first, second = values[y], values[y_size + y]
-        own = [first[:tok_rows, :], second[tok_rows:, :]]
-        far = [first[tok_rows:, :], second[:tok_rows, :]]
-        for x, (low, high) in enumerate((own, far)):
-            tokens = jnp.where(
-                place[1] == 0,
-                jnp.concatenate([low, high], axis=1),
-                jnp.concatenate([high, low], axis=1),
-            )
-            outs[x * y_size + y][...] = lax.dot_general(
-                tokens,
-                rows_all[...],
-                (((1,), (1,)), ((), ())),
-                preferred_element_type=jnp.float32,
-            ).astype(jnp.bfloat16)
+            flops=0,
+            bytes_accessed=4 * sum(math.prod(shape) for shape in shapes),
+            transcendentals=0,
+        ),
+    )(place, *arrays)
 
 
 def by_place(blocks, index):
@@ -244,49 +355,46 @@
     return lax.dynamic_slice_in_dim(jnp.concatenate([back, back], axis=0), start, size, 0)
 
 
-def plain_row_products(place, first, second, proj):
-    z_size, _, width = proj[0].shape
-    tok_rows = first[0].shape[0] // PAIR
-    cores = by_place(proj, place[3])
-    along = by_place([cores[:, k] for k in range(z_size)], place[0])
+def plain_row_products(place, token_rows, groups, proj):
+    width = proj[0].shape[2]
+    z_size = 2 * proj[0].shape[0]
+    cores = by_place(
+        [jnp.concatenate(proj[2 * c : 2 * c + 2], axis=0) for c in range(2)], place[3]
+    )
+    order = {bits: k for k, bits in enumerate(flips(z_size))}
+    along = jnp.stack([cores[:, order[k]] for k in range(z_size)])
+    along = jnp.take(along, jnp.arange(z_size, dtype=jnp.int32) ^ place[0], axis=0)
     every = along.reshape(-1, width)
-    outs = []
-    for x in range(PAIR):
-        for low, high in zip(first, second):
-            near, far = slice(0, tok_rows), slice(tok_rows, PAIR * tok_rows)
-            low, high = (low[near], high[far]) if x == 0 else (low[far], high[near])
-            tokens = jnp.where(
-                place[1] == 0,
-                jnp.concatenate([low, high], axis=1),
-                jnp.concatenate([high, low], axis=1),
-            )
-            outs.append(
-                jnp.dot(tokens, every.T, preferred_element_type=jnp.float32).astype(jnp.bfloat16)
-            )
-    return outs
-
-
-def row_products(place, first, second, proj):
-    z_size, rows, width = proj[0].shape
-    y_size = len(first)
-    tok_rows = first[0].shape[0] // PAIR
-    cols = z_size * len(proj) * rows
+    product = jnp.dot(token_rows, every.T, preferred_element_type=jnp.float32)
+    return jnp.split(product.astype(jnp.bfloat16), groups)
+
+
+def row_products(place, token_rows, groups, proj):
+    _, rows, width = proj[0].shape
+    z_size = 2 * proj[0].shape[0]
+    tok_rows = token_rows.shape[0] // groups
+    cols = 2 * z_size * rows
     if rows % 16 or cols % 128:
-        return plain_row_products(place, first, second, proj)
+        return plain_row_products(place, token_rows, groups, proj)
     whole = pl.BlockSpec(memory_space=pltpu.VMEM)
     shape = jax.ShapeDtypeStruct((tok_rows, cols), jnp.bfloat16)
     return pl.pallas_call(
-        functools.partial(row_kernel, z_size, y_size),
-        in_specs=[pl.BlockSpec(memory_space=pltpu.SMEM)] + [whole] * (2 * y_size + len(proj)),
-        out_specs=[whole] * (2 * y_size),
-        out_shape=[shape] * (2 * y_size),
-        scratch_shapes=[pltpu.VMEM((cols, width), jnp.bfloat16)],
+        functools.partial(row_kernel, z_size, groups),
+        in_specs=[pl.BlockSpec(memory_space=pltpu.SMEM), whole]
+        + [pl.BlockSpec(memory_space=pl.ANY)] * len(proj),
+        out_specs=[whole] * groups,
+        out_shape=[shape] * groups,
+        scratch_shapes=[
+            pltpu.VMEM((cols, width), jnp.bfloat16),
+            pltpu.SemaphoreType.DMA((2 * z_size,)),
+        ],
+        compiler_params=ROOM,
         cost_estimate=pl.CostEstimate(
-            flops=4 * y_size * tok_rows * width * cols,
-            bytes_accessed=2 * cols * (width + 2 * y_size * tok_rows),
+            flops=2 * groups * tok_rows * width * cols,
+            bytes_accessed=2 * cols * (width + groups * tok_rows),
             transcendentals=0,
         ),
-    )(place, *first, *second, *proj)
+    )(place, token_rows, *proj)
 
 
 def final_kernel(z_size, place, *refs):
@@ -323,12 +431,21 @@
         both = jnp.stack(both)
         both = jnp.where(place[1] == 0, both, both[::-1])
         return both.transpose(2, 3, 0, 1, 4).reshape(tokens, -1)
-    whole = pl.BlockSpec(memory_space=pltpu.VMEM)
+    steps = 2 if tokens % 64 == 0 else 1
+
+    def rows(array_cols):
+        return pl.BlockSpec((tokens // steps, array_cols), lambda i, place: (i, 0))
+
     return pl.pallas_call(
         functools.partial(final_kernel, z_size),
-        in_specs=[pl.BlockSpec(memory_space=pltpu.SMEM)] + [whole] * len(pieces),
-        out_specs=whole,
+        grid_spec=pltpu.PrefetchScalarGridSpec(
+            num_scalar_prefetch=1,
+            grid=(steps,),
+            in_specs=[rows(z_size * cols)] * len(pieces),
+            out_specs=rows(len(pieces) * z_size * cols),
+        ),
         out_shape=jax.ShapeDtypeStruct((tokens, len(pieces) * z_size * cols), jnp.bfloat16),
+        compiler_params=ROOM,
         cost_estimate=pl.CostEstimate(
             flops=0, bytes_accessed=4 * tokens * len(pieces) * z_size * cols, transcendentals=0
         ),
@@ -361,6 +478,19 @@
 def turned(index, step, size):
     moved = index + step
     return jnp.where(moved >= size, moved - size, moved)
+
+
+def z_bits(z_size):
+    assert z_size & (z_size - 1) == 0
+    return [1 << n for n in range(z_size.bit_length() - 2, -1, -1)]
+
+
+def flips(z_size):
+    bits = z_bits(z_size)
+    return [
+        functools.reduce(int.__xor__, [bit for n, bit in enumerate(bits) if k >> n & 1], 0)
+        for k in range(z_size)
+    ]
 
 
 def cut(value, index, dim):
@@ -392,24 +522,30 @@
     y_index, core_index = lax.axis_index("y"), lax.axis_index("core")
     place = jnp.stack([z_index, x_index, y_index, core_index]).astype(jnp.int32)
 
-    key_own, key_out, q_out, g_out = packed(place, key_vectors, queries, logp_grad)
+    key_room, key_out, q_out, g_out = packed(place, key_vectors, queries, logp_grad)
     key_far = shift(key_out, "x", 1)
     q_far = shift(q_out, "x", 1)
     g_far = shift(g_out, "x", 1)
-    key_block = jnp.concatenate([key_own, key_far], axis=0)
+    key_block = lax.dynamic_update_slice(key_room, key_far, (tok_rows, 0))
     key_blocks = [key_block] + [shift(key_block, "z", k, False) for k in range(1, z_size)]
-
     columns = attn_inputs.T.reshape(z_size, PAIR, y_size, core_size, shard_rows, tok_rows)
-    by_y = [cut(columns, y_index, 2)] + [
-        shift(cut(columns, turned(y_index, k, y_size), 2), "y", k)
-        for k in range(1, y_size)
-    ]
-    by_core = [
-        jnp.stack([cut(block, core_index, 2) for block in by_y]),
-        shift(jnp.stack([cut(block, 1 - core_index, 2) for block in by_y]), "core", 1),
-    ]
-    near_cols = jnp.stack([cut(block, x_index, 2) for block in by_core])
-    far_cols = shift(jnp.stack([cut(block, 1 - x_index, 2) for block in by_core]), "x", 1)
+    found = []
+    block = (z_size, core_size, shard_rows, tok_rows)
+    cuts = sliced(plane_kernel, place, [columns], [block] * (PAIR * y_size))
+    for x in range(PAIR):
+        for k in range(y_size):
+            piece = cuts[x * y_size + k]
+            if x or k:
+                pairs = [
+                    (a * y_size + b, (a + x) % PAIR * y_size + (b + k) % y_size)
+                    for a in range(PAIR)
+                    for b in range(y_size)
+                ]
+                piece = lax.ppermute(piece, ("x", "y"), pairs)
+            found.append(piece)
+    every = (PAIR * y_size, z_size, shard_rows, tok_rows)
+    near_cols, far_cols = sliced(core_kernel, place, found, [every] * 2)
+    far_cols = shift(far_cols, "core", 1)
 
     advantage = advantages(rewards, group_ids)
     rolls = jnp.arange(rewards.shape[0], dtype=jnp.int32)[None, :]
@@ -424,24 +560,21 @@
         len_roll[:, None],
         position[None, :],
         full_len,
-    ).reshape(tok_rows)
+    )
     coeff_far = shift(coeff, "x", 1)
 
     own_proj = lax.dynamic_slice_in_dim(value_proj, side_index * shard_rows, shard_rows, 0)
     own_proj = lax.optimization_barrier(own_proj)
-    own_rows = jnp.stack([own_proj] + [shift(own_proj, "z", k) for k in range(1, z_size)])
-    proj = [own_rows, shift(own_rows, "core", 1)]
-
-    parts = attention_parts(
-        place,
-        queries,
-        q_far,
-        logp_grad,
-        g_far,
-        coeff.reshape(tok_rows, 1),
-        coeff_far.reshape(tok_rows, 1),
-        key_blocks,
-    )
+    bits = z_bits(z_size)
+    known = own_proj[None]
+    for n, bit in enumerate(bits):
+        pairs = [(i, i ^ bit) for i in range(z_size)]
+        arrived = lax.ppermute(known, "z", pairs)
+        if n < len(bits) - 1:
+            known = jnp.concatenate([known, arrived], axis=0)
+    proj = [known, arrived, shift(known, "core", 1), shift(arrived, "core", 1)]
+
+    parts = attention_parts(place, queries, q_far, logp_grad, g_far, coeff, coeff_far, key_blocks)
     total = parts[0].astype(jnp.float32)
     for k in range(1, z_size):
         arrived = shift(parts[k], "z", -k, False)
@@ -462,25 +595,41 @@
     for piece in arrived:
         shard_grad = shard_grad + piece.astype(jnp.float32)
 
-    products = row_products(place, first_all[:y_size], second_all[:y_size], proj)
-    found = list(products)
+    products = row_products(place, pieces[z_size], PAIR * y_size, proj)
+    back = list(products)
     for k in range(1, y_size):
-        found[k] = shift(products[k], "y", -k)
-    found[y_size] = shift(products[y_size], "x", 1)
+        back[k] = shift(products[k], "y", -k)
+    back[y_size] = shift(products[y_size], "x", 1)
     for k in range(1, y_size):
         pairs = [
             (x * y_size + y, (1 - x) * y_size + (y - k) % y_size)
             for x in range(PAIR)
             for y in range(y_size)
         ]
-        found[y_size + k] = lax.ppermute(products[y_size + k], ("x", "y"), pairs)
-    input_grad = assembled(place, found, z_size)
+        back[y_size + k] = lax.ppermute(products[y_size + k], ("x", "y"), pairs)
+    input_grad = assembled(place, back, z_size)
 
     swap = jnp.concatenate([shard_grad[:, width // 2 :], shard_grad[:, : width // 2]], axis=1)
     new_rows, new_first, new_second = adam_rows(
         own_proj, jnp.where(x_index == 0, shard_grad, swap), first_moment, second_moment
     )
-    new_proj = lax.all_gather(new_rows, ("y", "core"), axis=0, tiled=True)
+    sides = [new_rows] + [shift(new_rows, "y", k) for k in range(1, y_size)]
+    others = [shift(block, "core", 1) for block in sides]
+    if y_size == 2:
+        columns = [
+            [jnp.where(y_index == 0, blocks[y], blocks[1 - y]) for y in range(2)]
+            for blocks in (sides, others)
+        ]
+    else:
+        columns = [list(by_place(blocks, y_index)) for blocks in (sides, others)]
+    new_proj = jnp.concatenate(
+        [
+            jnp.where(core_index == c, columns[0][y], columns[1][y])
+            for y in range(y_size)
+            for c in range(core_size)
+        ],
+        axis=0,
+    )
     return (input_grad, new_proj, new_first, new_second)
 
 

time: 125 us -> 109 us (0.87); the launches traced: 123 us -> 109 us
  blocking collectives: 7.9 us -> 0 us
  starting transfers between devices: 43.7 us -> 37.9 us
  local copies, waits for them, and re-layouts: 10.6 us -> 5.06 us
  waiting for transfers between devices: 35.9 us -> 40.3 us
    ppermute x29 -> x28, starting transfers between devices: 43.2 us -> 33.7 us  [shift(): return lax.ppermute(value, axis, pairs)]
    all_gather x1 -> x0, blocking collectives: 7.9 us -> none  [step(): new_proj = lax.all_gather(new_rows, ('y', 'core'), axis=0, tiled=True)]
    ppermute x29 -> x28, waiting for transfers between devices: 30.4 us -> 37 us  [shift(): return lax.ppermute(value, axis, pairs)]
    ppermute x1 -> x6, starting transfers between devices: 0.46 us -> 4.15 us  [the longest x3 3.49 us: step(): piece = lax.ppermute(piece, ('x', 'y'), pairs)]
    unnamed x53 -> x38, local copies, waits for them, and re-layouts: 6.17 us -> 3.54 us
    another operation x3 -> x0, local copies, waits for them, and re-layouts: 2.32 us -> none  [the longest x1 1.16 us: step(): jnp.stack([cut(block, 1 - x_index, 2) for block in by_core])]
    ppermute x1 -> x6, waiting for transfers between devices: 5.47 us -> 3.34 us  [the longest x3 3.33 us: step(): piece = lax.ppermute(piece, ('x', 'y'), pairs)]
    another operation x5 -> x0, other arithmetic: 2.01 us -> none  [the longest x1 0.92 us: step(): jnp.stack([own_proj] + [shift(own_proj, 'z', k) for k in range(1, z_size)])]
  transfers between devices with their start and end apart: 30 -> 34, of which waited for: 10 -> 12; matrix products, arithmetic and copies ran while one was open for 8% -> 5% of each run, Pallas kernels for 15% -> 15%
where the time goes in v1:
time: 109 us
  waiting for transfers between devices  40.3 us (37%)
  starting transfers between devices  37.9 us (35%)
  Pallas kernels  19.1 us (18%)
  other arithmetic  5.39 us (5%)
  local copies, waits for them, and re-layouts  5.06 us (5%)
    ppermute x28, waiting for transfers between devices, shift(): return lax.ppermute(value, axis, pairs)  37 us
    ppermute x28, starting transfers between devices, shift(): return lax.ppermute(value, axis, pairs)  33.7 us
    pallas_call x1, Pallas kernels, attention_parts(): pl.pallas_call(functools.partial(attention_kernel, slots, half), grid_spe...  5.2 us
    pallas_call x1, Pallas kernels, row_products(): pl.pallas_call(functools.partial(row_kernel, z_size, groups), in_specs=[p...  4.36 us
    unnamed x38, local copies, waits for them, and re-layouts  3.54 us
    ppermute x3, starting transfers between devices, step(): piece = lax.ppermute(piece, ('x', 'y'), pairs)  3.49 us
    ppermute x3, waiting for transfers between devices, step(): piece = lax.ppermute(piece, ('x', 'y'), pairs)  3.33 us
    pallas_call x1, Pallas kernels, packed(): pl.pallas_call(pack_kernel, grid_spec=pltpu.PrefetchScalarGridSpec(num_sc...  2.86 us
  transfers between devices with their start and end apart: 34, of which 12 were waited for; matrix products, arithmetic and copies ran while one was open for 5% of the time, Pallas kernels for 15%

profile of v1, /device:TPU:0, one launch (start us, length us, event | category | flops | bytes accessed | tf_op | source)
XLA Modules:
  0.0 108.8 jit_solution(10602147615086406615)
XLA Ops:
  0.7 0.6 pad_add_fusion.place
  1.3 2.9 %shard_map.149 = (bf16[256,256]{1,0:T(8,128)(2,1)}, bf16[128,256]{1,0:T(8,128)(2,1)}, bf16[128,1280]{1,0:T(8,128)(2,1)}, bf16[128,1280]{1,0:T(8,128)(2,1)}) custom-call(s32[4]{0:T(128)} %pad_add_fusion.place, bf16[128,512]{1,0:T(8,128)(2,1)} %k_far.1, bf16[128,512]{1,0:T(8,128)(2,1)} %k_far.1, bf16[128,2560]{1,0:T(8,128)(2,1)} %q_own.1, bf16[128,2560]{1,0:T(8,128)(2,1)} %g_own.1), custom_call_target="tpu_custom_call" | custom-call | bytes 1310720 | tf_op jit(solution)/shard_map/pallas_call | solution.py:154
  4.2 3.0 %collective-permute-start.4 = (bf16[128,1280]{1,0:T(8,128)(2,1)}, bf16[128,1280]{1,0:T(8,128)(2,1)}, u32[]{:S(2)}, u32[]{:S(2)}) collective-permute-start(bf16[128,1280]{1,0:T(8,128)(2,1)} %get-tuple-element.33), channel_id=1, source_target_pairs={{0,4},{4,0},{1,5},{5,1},{2,6},{6,2},{3,7},{7,3},{8,12},{12,8},{9,1... | collective-permute-start | bytes 983048 | tf_op jit(solution)/shard_map/ppermute | solution.py:475
  8.1 8.3 %collective-permute-done.7 = bf16[128,256]{1,0:T(8,128)(2,1)S(1)} collective-permute-done((bf16[128,256]{1,0:T(8,128)(2,1)}, bf16[128,256]{1,0:T(8,128)(2,1)S(1)}, u32[]{:S(2)}, u32[]{:S(2)}) %collective-permute-start.7) | collective-permute-done | bytes 65568 | tf_op jit(solution)/shard_map/ppermute | solution.py:475
  16.5 0.6 constant_dynamic-update-slice_fusion.refs_0_
  17.1 3.7 %collective-permute-start.8 = (bf16[256,256]{1,0:T(8,128)(2,1)}, bf16[256,256]{1,0:T(8,128)(2,1)S(1)}, u32[]{:S(2)}, u32[]{:S(2)}) collective-permute-start(bf16[256,256]{1,0:T(8,128)(2,1)} %constant_dynamic-update-slice_fusion.refs_0_), channel_id=1, source_target_pairs={{0,8},{8,16},{16,24},{1,9},{9,17},{17,25},{2,10},{10,18},{18,26},{... | collective-permute-start | bytes 393224 | tf_op jit(solution)/shard_map/ppermute | solution.py:475
  20.8 4.5 %collective-permute-start.9 = (bf16[256,256]{1,0:T(8,128)(2,1)}, bf16[256,256]{1,0:T(8,128)(2,1)S(1)}, u32[]{:S(2)}, u32[]{:S(2)}) collective-permute-start(bf16[256,256]{1,0:T(8,128)(2,1)} %constant_dynamic-update-slice_fusion.refs_0_), channel_id=1, source_target_pairs={{0,16},{8,24},{1,17},{9,25},{2,18},{10,26},{3,19},{11,27},{4,20},{... | collective-permute-start | bytes 393224 | tf_op jit(solution)/shard_map/ppermute | solution.py:475
  25.3 2.0 %collective-permute-start.10 = (bf16[256,256]{1,0:T(8,128)(2,1)}, bf16[256,256]{1,0:T(8,128)(2,1)}, u32[]{:S(2)}, u32[]{:S(2)}) collective-permute-start(bf16[256,256]{1,0:T(8,128)(2,1)} %constant_dynamic-update-slice_fusion.refs_0_), channel_id=1, source_target_pairs={{0,24},{1,25},{2,26},{3,27},{4,28},{5,29},{6,30},{7,31}} | collective-permute-start | bytes 393224 | tf_op jit(solution)/shard_map/ppermute | solution.py:475
  27.4 1.5 %collective-permute-start.6 = (f32[2,64]{1,0:T(2,128)S(1)}, f32[2,64]{1,0:T(2,128)S(1)}, u32[]{:S(2)}, u32[]{:S(2)}) collective-permute-start(f32[2,64]{1,0:T(2,128)S(1)} %and_select_fusion.c_own), channel_id=1, source_target_pairs={{0,4},{4,0},{1,5},{5,1},{2,6},{6,2},{3,7},{7,3},{8,12},{12,8},{9,1... | collective-permute-start | bytes 1544 | tf_op jit(solution)/shard_map/ppermute | solution.py:475
  28.9 2.1 %collective-permute-done.6.c_far = f32[2,64]{1,0:T(2,128)S(1)} collective-permute-done((f32[2,64]{1,0:T(2,128)S(1)}, f32[2,64]{1,0:T(2,128)S(1)}, u32[]{:S(2)}, u32[]{:S(2)}) %collective-permute-start.6) | collective-permute-done | bytes 544 | tf_op jit(solution)/shard_map/ppermute | solution.py:475
  30.9 1.5 %collective-permute-start.5 = (bf16[128,1280]{1,0:T(8,128)(2,1)}, bf16[128,1280]{1,0:T(8,128)(2,1)}, u32[]{:S(2)}, u32[]{:S(2)}) collective-permute-start(bf16[128,1280]{1,0:T(8,128)(2,1)} %get-tuple-element.34), channel_id=1, source_target_pairs={{0,4},{4,0},{1,5},{5,1},{2,6},{6,2},{3,7},{7,3},{8,12},{12,8},{9,1... | collective-permute-start | bytes 983048 | tf_op jit(solution)/shard_map/ppermute | solution.py:475
  32.4 0.8 copy.17
  33.2 1.6 %shard_map.147 = (bf16[4,2,160,128]{3,2,1,0:T(8,128)(2,1)S(1)}, bf16[4,2,160,128]{3,2,1,0:T(8,128)(2,1)}, bf16[4,2,160,128]{3,2,1,0:T(8,128)(2,1)}, bf16[4,2,160,128]{3,2,1,0:T(8,128)(2,1)}) custom-call(s32[4]{0:T(128)S(1)} %copy-done.5, bf16[4,2,2,2,160,128]{5,4,3,2,1,0:T(8,128)(2,1)S(1)} %bitcast.7), custom_call_target="tpu_custom_call" | custom-call | bytes 2621440 | tf_op jit(solution)/shard_map/pallas_call | solution.py:337
  34.8 0.7 copy-done.3
  35.5 1.5 %collective-permute-start = (bf16[4,2,160,128]{3,2,1,0:T(8,128)(2,1)}, bf16[4,2,160,128]{3,2,1,0:T(8,128)(2,1)S(1)}, u32[]{:S(2)}, u32[]{:S(2)}) collective-permute-start(bf16[4,2,160,128]{3,2,1,0:T(8,128)(2,1)} %get-tuple-element.28), channel_id=1, source_target_pairs={{0,2},{2,0},{4,6},{6,4},{1,3},{3,1},{5,7},{7,5},{8,10},{10,8},{12,... | collective-permute-start | bytes 983048 | tf_op jit(solution)/shard_map/ppermute | solution.py:544
  37.1 0.5 collective-permute-start.1
  37.6 1.4 %collective-permute-start.2 = (bf16[4,2,160,128]{3,2,1,0:T(8,128)(2,1)}, bf16[4,2,160,128]{3,2,1,0:T(8,128)(2,1)S(1)}, u32[]{:S(2)}, u32[]{:S(2)}) collective-permute-start(bf16[4,2,160,128]{3,2,1,0:T(8,128)(2,1)} %get-tuple-element.30), channel_id=1, source_target_pairs={{0,6},{2,4},{4,2},{6,0},{1,7},{3,5},{5,3},{7,1},{8,14},{10,12},{12... | collective-permute-start | bytes 983048 | tf_op jit(solution)/shard_map/ppermute | solution.py:544
  39.2 0.7 collective-permute-done.5.g_far
  39.9 0.9 copy-done.6
  40.8 5.2 %shard_map.150 = (bf16[256,256]{1,0:T(8,128)(2,1)S(1)}, bf16[256,256]{1,0:T(8,128)(2,1)S(1)}, bf16[256,256]{1,0:T(8,128)(2,1)S(1)}, bf16[256,256]{1,0:T(8,128)(2,1)S(1)}) custom-call(s32[4]{0:T(128)S(1)} %copy-done.5, bf16[128,2560]{1,0:T(8,128)(2,1)S(1)} %copy-done.1, bf16[128,1280]{1,0:T(8,128)(2,1)} %collective-permute-done.4.q_far, ...), custom_call_target="tpu_custom_call" | custom-call | flops 671088640 | bytes 1310720 | tf_op jit(solution)/shard_map/pallas_call | solution.py:113
  46.0 1.3 %collective-permute-start.13 = (bf16[256,256]{1,0:T(8,128)(2,1)S(1)}, bf16[256,256]{1,0:T(8,128)(2,1)S(1)}, u32[]{:S(2)}, u32[]{:S(2)}) collective-permute-start(bf16[256,256]{1,0:T(8,128)(2,1)S(1)} %get-tuple-element.40), channel_id=1, source_target_pairs={{24,0},{25,1},{26,2},{27,3},{28,4},{29,5},{30,6},{31,7}} | collective-permute-start | bytes 393224 | tf_op jit(solution)/shard_map/ppermute | solution.py:475
  47.3 1.3 %collective-permute-start.12 = (bf16[256,256]{1,0:T(8,128)(2,1)S(1)}, bf16[256,256]{1,0:T(8,128)(2,1)S(1)}, u32[]{:S(2)}, u32[]{:S(2)}) collective-permute-start(bf16[256,256]{1,0:T(8,128)(2,1)S(1)} %get-tuple-element.39), channel_id=1, source_target_pairs={{16,0},{24,8},{17,1},{25,9},{18,2},{26,10},{19,3},{27,11},{20,4},{... | collective-permute-start | bytes 393224 | tf_op jit(solution)/shard_map/ppermute | solution.py:475
  48.6 1.3 %collective-permute-start.11 = (bf16[256,256]{1,0:T(8,128)(2,1)S(1)}, bf16[256,256]{1,0:T(8,128)(2,1)S(1)}, u32[]{:S(2)}, u32[]{:S(2)}) collective-permute-start(bf16[256,256]{1,0:T(8,128)(2,1)S(1)} %get-tuple-element.38), channel_id=1, source_target_pairs={{8,0},{16,8},{24,16},{9,1},{17,9},{25,17},{10,2},{18,10},{26,18},{... | collective-permute-start | bytes 393224 | tf_op jit(solution)/shard_map/ppermute | solution.py:475
  49.9 3.3 %collective-permute-done.2.refs_3_ = bf16[4,2,160,128]{3,2,1,0:T(8,128)(2,1)S(1)} collective-permute-done((bf16[4,2,160,128]{3,2,1,0:T(8,128)(2,1)}, bf16[4,2,160,128]{3,2,1,0:T(8,128)(2,1)S(1)}, u32[]{:S(2)}, u32[]{:S(2)}) %collective-permute-start.2) | collective-permute-done | bytes 327712 | tf_op jit(solution)/shard_map/ppermute | solution.py:544
  53.2 0.6 shard_map.148
  54.1 0.7 collective-permute-done.13
  54.8 3.0 %collective-permute-done.12 = bf16[256,256]{1,0:T(8,128)(2,1)S(1)} collective-permute-done((bf16[256,256]{1,0:T(8,128)(2,1)S(1)}, bf16[256,256]{1,0:T(8,128)(2,1)S(1)}, u32[]{:S(2)}, u32[]{:S(2)}) %collective-permute-start.12) | collective-permute-done | bytes 131104 | tf_op jit(solution)/shard_map/ppermute | solution.py:475
  57.9 3.3 %collective-permute-start.14 = (bf16[256,256]{1,0:T(8,128)(2,1)S(1)}, bf16[256,256]{1,0:T(8,128)(2,1)S(1)}, u32[]{:S(2)}, u32[]{:S(2)}) collective-permute-start(bf16[256,256]{1,0:T(8,128)(2,1)S(1)} %add_convert_fusion.refs_0_), channel_id=1, source_target_pairs={{0,2},{2,0},{1,3},{3,1},{4,6},{6,4},{5,7},{7,5},{8,10},{10,8},{9,1... | collective-permute-start | bytes 393224 | tf_op jit(solution)/shard_map/ppermute | solution.py:475
  61.1 2.8 %collective-permute-start.17 = (bf16[256,256]{1,0:T(8,128)(2,1)S(1)}, bf16[256,256]{1,0:T(8,128)(2,1)S(1)}, u32[]{:S(2)}, u32[]{:S(2)}) collective-permute-start(bf16[256,256]{1,0:T(8,128)(2,1)S(1)} %add_convert_fusion.refs_0_), channel_id=1, source_target_pairs={{0,4},{4,0},{1,5},{5,1},{2,6},{6,2},{3,7},{7,3},{8,12},{12,8},{9,1... | collective-permute-start | bytes 393224 | tf_op jit(solution)/shard_map/ppermute | solution.py:475
  64.4 2.4 %collective-permute-done.17.refs_4_ = bf16[256,256]{1,0:T(8,128)(2,1)S(1)} collective-permute-done((bf16[256,256]{1,0:T(8,128)(2,1)S(1)}, bf16[256,256]{1,0:T(8,128)(2,1)S(1)}, u32[]{:S(2)}, u32[]{:S(2)}) %collective-permute-start.17) | collective-permute-done | bytes 131104 | tf_op jit(solution)/shard_map/ppermute | solution.py:475
  67.5 4.3 %collective-permute-done.18.refs_5_ = bf16[256,256]{1,0:T(8,128)(2,1)S(1)} collective-permute-done((bf16[256,256]{1,0:T(8,128)(2,1)S(1)}, bf16[256,256]{1,0:T(8,128)(2,1)S(1)}, u32[]{:S(2)}, u32[]{:S(2)}) %collective-permute-start.18) | collective-permute-done | bytes 131104 | tf_op jit(solution)/shard_map/ppermute | solution.py:475
  71.8 1.3 %collective-permute-done.20.refs_7_ = bf16[256,256]{1,0:T(8,128)(2,1)S(1)} collective-permute-done((bf16[256,256]{1,0:T(8,128)(2,1)S(1)}, bf16[256,256]{1,0:T(8,128)(2,1)S(1)}, u32[]{:S(2)}, u32[]{:S(2)}) %collective-permute-start.20) | collective-permute-done | bytes 131104 | tf_op jit(solution)/shard_map/ppermute | solution.py:475
  73.2 2.6 %shard_map.151 = (bf16[160,512]{1,0:T(8,128)(2,1)S(1)}, bf16[160,512]{1,0:T(8,128)(2,1)S(1)}, bf16[160,512]{1,0:T(8,128)(2,1)S(1)}, bf16[160,512]{1,0:T(8,128)(2,1)}, bf16[512,512]{1,0:T(8,128)(2,1)S(1)}) custom-call(s32[4]{0:T(128)S(1)} %copy-done.5, bf16[4,4,160,128]{3,2,1,0:T(8,128)(2,1)S(1)} %get-tuple-element.31.near, ...), custom_call_target="tpu_custom_call" | custom-call | flops 671088640 | bytes 2621440 | tf_op jit(solution)/shard_map/pallas_call | solution.py:264
  75.8 0.8 copy-done.7
  76.6 2.1 %collective-permute-start.29 = (bf16[160,512]{1,0:T(8,128)(2,1)S(1)}, bf16[160,512]{1,0:T(8,128)(2,1)}, u32[]{:S(2)}, u32[]{:S(2)}) collective-permute-start(bf16[160,512]{1,0:T(8,128)(2,1)S(1)} %get-tuple-element.48), channel_id=1, source_target_pairs={{0,16},{8,24},{16,0},{24,8},{1,17},{9,25},{17,1},{25,9},{2,18},{10... | collective-permute-start | bytes 491528 | tf_op jit(solution)/shard_map/ppermute | solution.py:475
  78.8 0.8 collective-permute-start.28
  79.6 1.0 copy-done.8
  80.6 4.4 %shard_map.152 = (bf16[128,1280]{1,0:T(8,128)(2,1)S(1)}, bf16[128,1280]{1,0:T(8,128)(2,1)}, bf16[128,1280]{1,0:T(8,128)(2,1)S(1)}, bf16[128,1280]{1,0:T(8,128)(2,1)S(1)}) custom-call(s32[4]{0:T(128)S(1)} %copy-done.5, bf16[512,512]{1,0:T(8,128)(2,1)S(1)} %copy-done.8, bf16[2,160,512]{2,1,0:T(8,128)(2,1)S(1)} %pad_maximum_fusion.1.refs_0_, ...), custom_call_target="tpu_custom_call" | custom-call | flops 671088640 | bytes 2621440 | tf_op jit(solution)/shard_map/pallas_call | solution.py:381
  85.0 0.6 collective-permute-start.25
  85.6 2.5 %collective-permute-start.26 = (bf16[128,1280]{1,0:T(8,128)(2,1)S(1)}, bf16[128,1280]{1,0:T(8,128)(2,1)S(1)}, u32[]{:S(2)}, u32[]{:S(2)}) collective-permute-start(bf16[128,1280]{1,0:T(8,128)(2,1)S(1)} %get-tuple-element.44), channel_id=1, source_target_pairs={{0,4},{4,0},{1,5},{5,1},{2,6},{6,2},{3,7},{7,3},{8,12},{12,8},{9,1... | collective-permute-start | bytes 983048 | tf_op jit(solution)/shard_map/ppermute | solution.py:475
  88.6 5.3 %collective-permute-done.29 = bf16[160,512]{1,0:T(8,128)(2,1)} collective-permute-done((bf16[160,512]{1,0:T(8,128)(2,1)S(1)}, bf16[160,512]{1,0:T(8,128)(2,1)}, u32[]{:S(2)}, u32[]{:S(2)}) %collective-permute-start.29) | collective-permute-done | bytes 163872 | tf_op jit(solution)/shard_map/ppermute | solution.py:475
  93.8 1.2 %convert_add_fusion = f32[160,512]{1,0:T(8,128)S(1)} fusion(bf16[160,512]{1,0:T(8,128)(2,1)} %collective-permute-done.30, bf16[160,512]{1,0:T(8,128)(2,1)} %collective-permute-done.29, bf16[160,512]{1,0:T(8,128)(2,1)} %collective-permute-done.28, bf16[160,512]{1,0:T(8,128)(2,1)S(1)} %get-tuple-element.46), kind=kLoop, calls=%fused_computation.11 | loop fusion | flops 573440 | bytes 983040 | tf_op jit(solution)/shard_map/add | solution.py:596
  95.1 0.8 fusion.5
  95.8 1.0 fusion.4
  96.8 0.5 collective-permute-start.31
  97.3 8.7 %collective-permute-done.31 = bf16[160,512]{1,0:T(8,128)(2,1)S(1)} collective-permute-done((bf16[160,512]{1,0:T(8,128)(2,1)S(1)}, bf16[160,512]{1,0:T(8,128)(2,1)S(1)}, u32[]{:S(2)}, u32[]{:S(2)}) %collective-permute-start.31) | collective-permute-done | bytes 163872 | tf_op jit(solution)/shard_map/ppermute | solution.py:475
  106.0 1.8 %shard_map.153 = bf16[128,5120]{1,0:T(8,128)(2,1)} custom-call(s32[4]{0:T(128)S(1)} %copy-done.5, bf16[128,1280]{1,0:T(8,128)(2,1)S(1)} %get-tuple-element.42.refs_0_, bf16[128,1280]{1,0:T(8,128)(2,1)S(1)} %collective-permute-done.25.refs_1_, bf16[128,1280]{1,0:T(8,128)(2,1)S(1)} %collective-permute-done.26.refs_2_, ...), custom_call_target="tpu_custom_call" | custom-call | bytes 2621440 | tf_op jit(solution)/shard_map/pallas_call | solution.py:439
  107.9 0.9 pad_maximum_fusion
  (90 shorter events, 3.3 us)
Async XLA Ops:
  0.6 38.4 %copy-start = (bf16[640,512]{1,0:T(8,128)(2,1)S(1)}, bf16[640,512]{1,0:T(8,128)(2,1)}, u32[]{:S(2)}) copy-start(bf16[640,512]{1,0:T(8,128)(2,1)} %param.21) | copy-start | bytes 1966084
  0.6 6.6 %copy-start.16 = (f32[128]{0:T(128)S(1)}, f32[128]{0:T(128)}, u32[]{:S(2)}) copy-start(f32[128]{0:T(128)} %param.16) | copy-start | bytes 1540
  0.7 6.6 %copy-start.17 = (f32[128]{0:T(128)S(1)}, f32[128]{0:T(128)}, u32[]{:S(2)}) copy-start(f32[128]{0:T(128)} %param.17) | copy-start | bytes 1540
  0.7 6.6 %copy-start.18 = (s32[8]{0:T(128)S(1)}, s32[8]{0:T(128)}, u32[]{:S(2)}) copy-start(s32[8]{0:T(128)} %param.20) | copy-start | bytes 100
  0.7 6.8 %copy-start.15 = (f32[8]{0:T(128)S(1)}, f32[8]{0:T(128)}, u32[]{:S(2)}) copy-start(f32[8]{0:T(128)} %param.18) | copy-start | bytes 100
  0.7 6.8 %copy-start.14 = (s32[8]{0:T(128)S(1)}, s32[8]{0:T(128)}, u32[]{:S(2)}) copy-start(s32[8]{0:T(128)} %param.19) | copy-start | bytes 100
  0.7 31.7 %copy-start.11 = (bf16[128,5120]{1,0:T(8,128)(2,1)S(1)}, bf16[128,5120]{1,0:T(8,128)(2,1)}, u32[]{:S(2)}) copy-start(bf16[128,5120]{1,0:T(8,128)(2,1)} %param.12) | copy-start | bytes 3932164
  4.2 34.9 %collective-permute-start.4 = (bf16[128,1280]{1,0:T(8,128)(2,1)}, bf16[128,1280]{1,0:T(8,128)(2,1)}, u32[]{:S(2)}, u32[]{:S(2)}) collective-permute-start(bf16[128,1280]{1,0:T(8,128)(2,1)} %get-tuple-element.33), channel_id=1, source_target_pairs={{0,4},{4,0},{1,5},{5,1},{2,6},{6,2},{3,7},{7,3},{8,12},{12,8},{9,1... | collective-permute-start | bytes 983048 | tf_op jit(solution)/shard_map/ppermute | solution.py:475
  7.1 9.3 %collective-permute-start.7 = (bf16[128,256]{1,0:T(8,128)(2,1)}, bf16[128,256]{1,0:T(8,128)(2,1)S(1)}, u32[]{:S(2)}, u32[]{:S(2)}) collective-permute-start(bf16[128,256]{1,0:T(8,128)(2,1)} %get-tuple-element.36), channel_id=1, source_target_pairs={{0,4},{4,0},{1,5},{5,1},{2,6},{6,2},{3,7},{7,3},{8,12},{12,8},{9,1... | collective-permute-start | bytes 196616 | tf_op jit(solution)/shard_map/ppermute | solution.py:475
  17.1 18.5 %collective-permute-start.8 = (bf16[256,256]{1,0:T(8,128)(2,1)}, bf16[256,256]{1,0:T(8,128)(2,1)S(1)}, u32[]{:S(2)}, u32[]{:S(2)}) collective-permute-start(bf16[256,256]{1,0:T(8,128)(2,1)} %constant_dynamic-update-slice_fusion.refs_0_), channel_id=1, source_target_pairs={{0,8},{8,16},{16,24},{1,9},{9,17},{17,25},{2,10},{10,18},{18,26},{... | collective-permute-start | bytes 393224 | tf_op jit(solution)/shard_map/ppermute | solution.py:475
  20.8 16.2 %collective-permute-start.9 = (bf16[256,256]{1,0:T(8,128)(2,1)}, bf16[256,256]{1,0:T(8,128)(2,1)S(1)}, u32[]{:S(2)}, u32[]{:S(2)}) collective-permute-start(bf16[256,256]{1,0:T(8,128)(2,1)} %constant_dynamic-update-slice_fusion.refs_0_), channel_id=1, source_target_pairs={{0,16},{8,24},{1,17},{9,25},{2,18},{10,26},{3,19},{11,27},{4,20},{... | collective-permute-start | bytes 393224 | tf_op jit(solution)/shard_map/ppermute | solution.py:475
  25.3 12.3 %collective-permute-start.10 = (bf16[256,256]{1,0:T(8,128)(2,1)}, bf16[256,256]{1,0:T(8,128)(2,1)}, u32[]{:S(2)}, u32[]{:S(2)}) collective-permute-start(bf16[256,256]{1,0:T(8,128)(2,1)} %constant_dynamic-update-slice_fusion.refs_0_), channel_id=1, source_target_pairs={{0,24},{1,25},{2,26},{3,27},{4,28},{5,29},{6,30},{7,31}} | collective-permute-start | bytes 393224 | tf_op jit(solution)/shard_map/ppermute | solution.py:475
  27.4 3.6 %collective-permute-start.6 = (f32[2,64]{1,0:T(2,128)S(1)}, f32[2,64]{1,0:T(2,128)S(1)}, u32[]{:S(2)}, u32[]{:S(2)}) collective-permute-start(f32[2,64]{1,0:T(2,128)S(1)} %and_select_fusion.c_own), channel_id=1, source_target_pairs={{0,4},{4,0},{1,5},{5,1},{2,6},{6,2},{3,7},{7,3},{8,12},{12,8},{9,1... | collective-permute-start | bytes 1544 | tf_op jit(solution)/shard_map/ppermute | solution.py:475
  30.9 8.9 %collective-permute-start.5 = (bf16[128,1280]{1,0:T(8,128)(2,1)}, bf16[128,1280]{1,0:T(8,128)(2,1)}, u32[]{:S(2)}, u32[]{:S(2)}) collective-permute-start(bf16[128,1280]{1,0:T(8,128)(2,1)} %get-tuple-element.34), channel_id=1, source_target_pairs={{0,4},{4,0},{1,5},{5,1},{2,6},{6,2},{3,7},{7,3},{8,12},{12,8},{9,1... | collective-permute-start | bytes 983048 | tf_op jit(solution)/shard_map/ppermute | solution.py:475
  33.2 6.6 %copy-start.1 = (bf16[128,2560]{1,0:T(8,128)(2,1)S(1)}, bf16[128,2560]{1,0:T(8,128)(2,1)}, u32[]{:S(2)}) copy-start(bf16[128,2560]{1,0:T(8,128)(2,1)} %q_own.1) | copy-start | bytes 1966084
  33.2 6.6 %copy-start.2 = (bf16[128,2560]{1,0:T(8,128)(2,1)S(1)}, bf16[128,2560]{1,0:T(8,128)(2,1)}, u32[]{:S(2)}) copy-start(bf16[128,2560]{1,0:T(8,128)(2,1)} %g_own.1) | copy-start | bytes 1966084
  35.5 11.7 %collective-permute-start = (bf16[4,2,160,128]{3,2,1,0:T(8,128)(2,1)}, bf16[4,2,160,128]{3,2,1,0:T(8,128)(2,1)S(1)}, u32[]{:S(2)}, u32[]{:S(2)}) collective-permute-start(bf16[4,2,160,128]{3,2,1,0:T(8,128)(2,1)} %get-tuple-element.28), channel_id=1, source_target_pairs={{0,2},{2,0},{4,6},{6,4},{1,3},{3,1},{5,7},{7,5},{8,10},{10,8},{12,... | collective-permute-start | bytes 983048 | tf_op jit(solution)/shard_map/ppermute | solution.py:544
  37.1 11.5 %collective-permute-start.1 = (bf16[4,2,160,128]{3,2,1,0:T(8,128)(2,1)}, bf16[4,2,160,128]{3,2,1,0:T(8,128)(2,1)S(1)}, u32[]{:S(2)}, u32[]{:S(2)}) collective-permute-start(bf16[4,2,160,128]{3,2,1,0:T(8,128)(2,1)} %get-tuple-element.29), channel_id=1, source_target_pairs={{0,4},{2,6},{4,0},{6,2},{1,5},{3,7},{5,1},{7,3},{8,12},{10,14},{12... | collective-permute-start | bytes 983048 | tf_op jit(solution)/shard_map/ppermute | solution.py:544
  37.6 15.6 %collective-permute-start.2 = (bf16[4,2,160,128]{3,2,1,0:T(8,128)(2,1)}, bf16[4,2,160,128]{3,2,1,0:T(8,128)(2,1)S(1)}, u32[]{:S(2)}, u32[]{:S(2)}) collective-permute-start(bf16[4,2,160,128]{3,2,1,0:T(8,128)(2,1)} %get-tuple-element.30), channel_id=1, source_target_pairs={{0,6},{2,4},{4,2},{6,0},{1,7},{3,5},{5,3},{7,1},{8,14},{10,12},{12... | collective-permute-start | bytes 983048 | tf_op jit(solution)/shard_map/ppermute | solution.py:544
  39.1 14.9 %copy-start.9 = (bf16[160,512]{1,0:T(8,128)(2,1)}, bf16[160,512]{1,0:T(8,128)(2,1)S(1)}, u32[]{:S(2)}) copy-start(bf16[160,512]{1,0:T(8,128)(2,1)S(1)} %constant_dynamic-slice_fusion) | copy-start | bytes 491524
  39.1 14.1 %copy-start.4 = (bf16[4,2,160,128]{3,2,1,0:T(8,128)(2,1)S(1)}, bf16[4,2,160,128]{3,2,1,0:T(8,128)(2,1)}, u32[]{:S(2)}) copy-start(bf16[4,2,160,128]{3,2,1,0:T(8,128)(2,1)} %copy-done.3) | copy-start | bytes 983044
  39.1 14.9 %collective-permute-start.21 = (bf16[1,160,512]{2,1,0:T(8,128)(2,1)S(1)}, bf16[1,160,512]{2,1,0:T(8,128)(2,1)S(1)}, u32[]{:S(2)}, u32[]{:S(2)}) collective-permute-start(bf16[1,160,512]{2,1,0:T(8,128)(2,1)S(1)} %bitcast.8), channel_id=1, source_target_pairs={{0,16},{8,24},{16,0},{24,8},{1,17},{9,25},{17,1},{25,9},{2,18},{10... | collective-permute-start | bytes 491528 | tf_op jit(solution)/shard_map/ppermute | solution.py:572
  46.0 8.8 %collective-permute-start.13 = (bf16[256,256]{1,0:T(8,128)(2,1)S(1)}, bf16[256,256]{1,0:T(8,128)(2,1)S(1)}, u32[]{:S(2)}, u32[]{:S(2)}) collective-permute-start(bf16[256,256]{1,0:T(8,128)(2,1)S(1)} %get-tuple-element.40), channel_id=1, source_target_pairs={{24,0},{25,1},{26,2},{27,3},{28,4},{29,5},{30,6},{31,7}} | collective-permute-start | bytes 393224 | tf_op jit(solution)/shard_map/ppermute | solution.py:475
  47.3 10.5 %collective-permute-start.12 = (bf16[256,256]{1,0:T(8,128)(2,1)S(1)}, bf16[256,256]{1,0:T(8,128)(2,1)S(1)}, u32[]{:S(2)}, u32[]{:S(2)}) collective-permute-start(bf16[256,256]{1,0:T(8,128)(2,1)S(1)} %get-tuple-element.39), channel_id=1, source_target_pairs={{16,0},{24,8},{17,1},{25,9},{18,2},{26,10},{19,3},{27,11},{20,4},{... | collective-permute-start | bytes 393224 | tf_op jit(solution)/shard_map/ppermute | solution.py:475
  48.6 9.2 %collective-permute-start.11 = (bf16[256,256]{1,0:T(8,128)(2,1)S(1)}, bf16[256,256]{1,0:T(8,128)(2,1)S(1)}, u32[]{:S(2)}, u32[]{:S(2)}) collective-permute-start(bf16[256,256]{1,0:T(8,128)(2,1)S(1)} %get-tuple-element.38), channel_id=1, source_target_pairs={{8,0},{16,8},{24,16},{9,1},{17,9},{25,17},{10,2},{18,10},{26,18},{... | collective-permute-start | bytes 393224 | tf_op jit(solution)/shard_map/ppermute | solution.py:475
  53.9 19.3 %collective-permute-start.3 = (bf16[4,4,160,128]{3,2,1,0:T(8,128)(2,1)S(1)}, bf16[4,4,160,128]{3,2,1,0:T(8,128)(2,1)S(1)}, u32[]{:S(2)}, u32[]{:S(2)}) collective-permute-start(bf16[4,4,160,128]{3,2,1,0:T(8,128)(2,1)S(1)} %get-tuple-element.32), channel_id=1, source_target_pairs={{0,1},{1,0},{2,3},{3,2},{4,5},{5,4},{6,7},{7,6},{8,9},{9,8},{10,11... | collective-permute-start | bytes 1966088 | tf_op jit(solution)/shard_map/ppermute | solution.py:475
  54.0 12.9 %collective-permute-start.22 = (bf16[2,160,512]{2,1,0:T(8,128)(2,1)S(1)}, bf16[2,160,512]{2,1,0:T(8,128)(2,1)S(1)}, u32[]{:S(2)}, u32[]{:S(2)}) collective-permute-start(bf16[2,160,512]{2,1,0:T(8,128)(2,1)S(1)} %pad_maximum_fusion.1.refs_0_), channel_id=1, source_target_pairs={{0,8},{8,0},{16,24},{24,16},{1,9},{9,1},{17,25},{25,17},{2,10},{10... | collective-permute-start | bytes 983048 | tf_op jit(solution)/shard_map/ppermute | solution.py:572
  57.9 6.2 %collective-permute-start.14 = (bf16[256,256]{1,0:T(8,128)(2,1)S(1)}, bf16[256,256]{1,0:T(8,128)(2,1)S(1)}, u32[]{:S(2)}, u32[]{:S(2)}) collective-permute-start(bf16[256,256]{1,0:T(8,128)(2,1)S(1)} %add_convert_fusion.refs_0_), channel_id=1, source_target_pairs={{0,2},{2,0},{1,3},{3,1},{4,6},{6,4},{5,7},{7,5},{8,10},{10,8},{9,1... | collective-permute-start | bytes 393224 | tf_op jit(solution)/shard_map/ppermute | solution.py:475
  61.1 5.7 %collective-permute-start.17 = (bf16[256,256]{1,0:T(8,128)(2,1)S(1)}, bf16[256,256]{1,0:T(8,128)(2,1)S(1)}, u32[]{:S(2)}, u32[]{:S(2)}) collective-permute-start(bf16[256,256]{1,0:T(8,128)(2,1)S(1)} %add_convert_fusion.refs_0_), channel_id=1, source_target_pairs={{0,4},{4,0},{1,5},{5,1},{2,6},{6,2},{3,7},{7,3},{8,12},{12,8},{9,1... | collective-permute-start | bytes 393224 | tf_op jit(solution)/shard_map/ppermute | solution.py:475
  63.9 3.0 %collective-permute-start.15 = (bf16[256,256]{1,0:T(8,128)(2,1)S(1)}, bf16[256,256]{1,0:T(8,128)(2,1)S(1)}, u32[]{:S(2)}, u32[]{:S(2)}) collective-permute-start(bf16[256,256]{1,0:T(8,128)(2,1)S(1)} %add_convert_fusion.refs_0_), channel_id=1, source_target_pairs={{0,1},{1,0},{2,3},{3,2},{4,5},{5,4},{6,7},{7,6},{8,9},{9,8},{10,11... | collective-permute-start | bytes 393224 | tf_op jit(solution)/shard_map/ppermute | solution.py:475
  64.1 3.4 %collective-permute-start.16 = (bf16[256,256]{1,0:T(8,128)(2,1)S(1)}, bf16[256,256]{1,0:T(8,128)(2,1)S(1)}, u32[]{:S(2)}, u32[]{:S(2)}) collective-permute-start(bf16[256,256]{1,0:T(8,128)(2,1)S(1)} %collective-permute-done.14.refs_1_), channel_id=1, source_target_pairs={{0,1},{1,0},{2,3},{3,2},{4,5},{5,4},{6,7},{7,6},{8,9},{9,8},{10,11... | collective-permute-start | bytes 393224 | tf_op jit(solution)/shard_map/ppermute | solution.py:475
  66.9 5.0 %collective-permute-start.18 = (bf16[256,256]{1,0:T(8,128)(2,1)S(1)}, bf16[256,256]{1,0:T(8,128)(2,1)S(1)}, u32[]{:S(2)}, u32[]{:S(2)}) collective-permute-start(bf16[256,256]{1,0:T(8,128)(2,1)S(1)} %collective-permute-done.17.refs_4_), channel_id=1, source_target_pairs={{0,2},{2,0},{1,3},{3,1},{4,6},{6,4},{5,7},{7,5},{8,10},{10,8},{9,1... | collective-permute-start | bytes 393224 | tf_op jit(solution)/shard_map/ppermute | solution.py:475
  66.9 12.6 %collective-permute-start.23 = (bf16[2,160,512]{2,1,0:T(8,128)(2,1)S(1)}, bf16[2,160,512]{2,1,0:T(8,128)(2,1)S(1)}, u32[]{:S(2)}, u32[]{:S(2)}) collective-permute-start(bf16[2,160,512]{2,1,0:T(8,128)(2,1)S(1)} %pad_maximum_fusion.1.refs_0_), channel_id=1, source_target_pairs={{0,1},{1,0},{2,3},{3,2},{4,5},{5,4},{6,7},{7,6},{8,9},{9,8},{10,11... | collective-permute-start | bytes 983048 | tf_op jit(solution)/shard_map/ppermute | solution.py:475
  66.9 12.6 %collective-permute-start.24 = (bf16[2,160,512]{2,1,0:T(8,128)(2,1)S(1)}, bf16[2,160,512]{2,1,0:T(8,128)(2,1)}, u32[]{:S(2)}, u32[]{:S(2)}) collective-permute-start(bf16[2,160,512]{2,1,0:T(8,128)(2,1)S(1)} %collective-permute-done.22.refs_1_), channel_id=1, source_target_pairs={{0,1},{1,0},{2,3},{3,2},{4,5},{5,4},{6,7},{7,6},{8,9},{9,8},{10,11... | collective-permute-start | bytes 983048 | tf_op jit(solution)/shard_map/ppermute | solution.py:475
  67.5 4.4 %collective-permute-start.19 = (bf16[256,256]{1,0:T(8,128)(2,1)S(1)}, bf16[256,256]{1,0:T(8,128)(2,1)S(1)}, u32[]{:S(2)}, u32[]{:S(2)}) collective-permute-start(bf16[256,256]{1,0:T(8,128)(2,1)S(1)} %collective-permute-done.17.refs_4_), channel_id=1, source_target_pairs={{0,1},{1,0},{2,3},{3,2},{4,5},{5,4},{6,7},{7,6},{8,9},{9,8},{10,11... | collective-permute-start | bytes 393224 | tf_op jit(solution)/shard_map/ppermute | solution.py:475
  71.8 1.3 %collective-permute-start.20 = (bf16[256,256]{1,0:T(8,128)(2,1)S(1)}, bf16[256,256]{1,0:T(8,128)(2,1)S(1)}, u32[]{:S(2)}, u32[]{:S(2)}) collective-permute-start(bf16[256,256]{1,0:T(8,128)(2,1)S(1)} %collective-permute-done.18.refs_5_), channel_id=1, source_target_pairs={{0,1},{1,0},{2,3},{3,2},{4,5},{5,4},{6,7},{7,6},{8,9},{9,8},{10,11... | collective-permute-start | bytes 393224 | tf_op jit(solution)/shard_map/ppermute | solution.py:475
  76.6 11.4 %collective-permute-start.30 = (bf16[160,512]{1,0:T(8,128)(2,1)}, bf16[160,512]{1,0:T(8,128)(2,1)}, u32[]{:S(2)}, u32[]{:S(2)}) collective-permute-start(bf16[160,512]{1,0:T(8,128)(2,1)} %get-tuple-element.49), channel_id=1, source_target_pairs={{0,24},{8,0},{16,8},{24,16},{1,25},{9,1},{17,9},{25,17},{2,26},{10... | collective-permute-start | bytes 491528 | tf_op jit(solution)/shard_map/ppermute | solution.py:475
  76.6 17.2 %collective-permute-start.29 = (bf16[160,512]{1,0:T(8,128)(2,1)S(1)}, bf16[160,512]{1,0:T(8,128)(2,1)}, u32[]{:S(2)}, u32[]{:S(2)}) collective-permute-start(bf16[160,512]{1,0:T(8,128)(2,1)S(1)} %get-tuple-element.48), channel_id=1, source_target_pairs={{0,16},{8,24},{16,0},{24,8},{1,17},{9,25},{17,1},{25,9},{2,18},{10... | collective-permute-start | bytes 491528 | tf_op jit(solution)/shard_map/ppermute | solution.py:475
  78.8 15.1 %collective-permute-start.28 = (bf16[160,512]{1,0:T(8,128)(2,1)S(1)}, bf16[160,512]{1,0:T(8,128)(2,1)}, u32[]{:S(2)}, u32[]{:S(2)}) collective-permute-start(bf16[160,512]{1,0:T(8,128)(2,1)S(1)} %get-tuple-element.47), channel_id=1, source_target_pairs={{0,8},{8,16},{16,24},{24,0},{1,9},{9,17},{17,25},{25,1},{2,10},{10... | collective-permute-start | bytes 491528 | tf_op jit(solution)/shard_map/ppermute | solution.py:475
  85.0 10.1 %copy-start.12 = (bf16[160,512]{1,0:T(8,128)(2,1)S(1)}, bf16[160,512]{1,0:T(8,128)(2,1)}, u32[]{:S(2)}) copy-start(bf16[160,512]{1,0:T(8,128)(2,1)} %param.23) | copy-start | bytes 491524
  85.0 21.0 %collective-permute-start.25 = (bf16[128,1280]{1,0:T(8,128)(2,1)}, bf16[128,1280]{1,0:T(8,128)(2,1)S(1)}, u32[]{:S(2)}, u32[]{:S(2)}) collective-permute-start(bf16[128,1280]{1,0:T(8,128)(2,1)} %get-tuple-element.43), channel_id=1, source_target_pairs={{0,2},{2,0},{1,3},{3,1},{4,6},{6,4},{5,7},{7,5},{8,10},{10,8},{9,1... | collective-permute-start | bytes 983048 | tf_op jit(solution)/shard_map/ppermute | solution.py:475
  85.6 20.4 %collective-permute-start.26 = (bf16[128,1280]{1,0:T(8,128)(2,1)S(1)}, bf16[128,1280]{1,0:T(8,128)(2,1)S(1)}, u32[]{:S(2)}, u32[]{:S(2)}) collective-permute-start(bf16[128,1280]{1,0:T(8,128)(2,1)S(1)} %get-tuple-element.44), channel_id=1, source_target_pairs={{0,4},{4,0},{1,5},{5,1},{2,6},{6,2},{3,7},{7,3},{8,12},{12,8},{9,1... | collective-permute-start | bytes 983048 | tf_op jit(solution)/shard_map/ppermute | solution.py:475
  88.1 18.0 %collective-permute-start.27 = (bf16[128,1280]{1,0:T(8,128)(2,1)S(1)}, bf16[128,1280]{1,0:T(8,128)(2,1)S(1)}, u32[]{:S(2)}, u32[]{:S(2)}) collective-permute-start(bf16[128,1280]{1,0:T(8,128)(2,1)S(1)} %get-tuple-element.45), channel_id=1, source_target_pairs={{0,6},{2,4},{4,2},{6,0},{1,7},{3,5},{5,3},{7,1},{8,14},{10,12},{12... | collective-permute-start | bytes 983048 | tf_op jit(solution)/shard_map/ppermute | solution.py:609
  93.8 2.0 %copy-start.10 = (bf16[160,512]{1,0:T(8,128)(2,1)S(1)}, bf16[160,512]{1,0:T(8,128)(2,1)}, u32[]{:S(2)}) copy-start(bf16[160,512]{1,0:T(8,128)(2,1)} %copy-done.9) | copy-start | bytes 491524
  93.8 2.0 %copy-start.13 = (bf16[160,512]{1,0:T(8,128)(2,1)S(1)}, bf16[160,512]{1,0:T(8,128)(2,1)}, u32[]{:S(2)}) copy-start(bf16[160,512]{1,0:T(8,128)(2,1)} %param.22) | copy-start | bytes 491524
  96.8 9.2 %collective-permute-start.31 = (bf16[160,512]{1,0:T(8,128)(2,1)S(1)}, bf16[160,512]{1,0:T(8,128)(2,1)S(1)}, u32[]{:S(2)}, u32[]{:S(2)}) collective-permute-start(bf16[160,512]{1,0:T(8,128)(2,1)S(1)} %get-tuple-element.61), channel_id=1, source_target_pairs={{0,2},{2,0},{1,3},{3,1},{4,6},{6,4},{5,7},{7,5},{8,10},{10,8},{9,1... | collective-permute-start | bytes 491528 | tf_op jit(solution)/shard_map/ppermute | solution.py:475
  97.3 10.5 %collective-permute-start.32 = (bf16[160,512]{1,0:T(8,128)(2,1)S(1)}, bf16[160,512]{1,0:T(8,128)(2,1)S(1)}, u32[]{:S(2)}, u32[]{:S(2)}) collective-permute-start(bf16[160,512]{1,0:T(8,128)(2,1)S(1)} %get-tuple-element.61), channel_id=1, source_target_pairs={{0,1},{1,0},{2,3},{3,2},{4,5},{5,4},{6,7},{7,6},{8,9},{9,8},{10,11... | collective-permute-start | bytes 491528 | tf_op jit(solution)/shard_map/ppermute | solution.py:475
  106.0 1.8 %collective-permute-start.33 = (bf16[160,512]{1,0:T(8,128)(2,1)S(1)}, bf16[160,512]{1,0:T(8,128)(2,1)S(1)}, u32[]{:S(2)}, u32[]{:S(2)}) collective-permute-start(bf16[160,512]{1,0:T(8,128)(2,1)S(1)} %collective-permute-done.31), channel_id=1, source_target_pairs={{0,1},{1,0},{2,3},{3,2},{4,5},{5,4},{6,7},{7,6},{8,9},{9,8},{10,11... | collective-permute-start | bytes 491528 | tf_op jit(solution)/shard_map/ppermute | solution.py:475
  (5 other events, 4.3 us)
